TPU v7x, 32 devices: a whole 2x2x4 slice. The times are simulated.
32 devices in a mesh: dp: 8 (over y, x, core), seq: 4 (over z).
Axes of the slice: x: 2, y: 2, z: 4, core: 2. Of those that a mesh axis runs over, the one named last changes fastest.
Arguments:
- tokens: bfloat16 [8, 2048, 768], P('dp', 'seq'), may hold values from -6 to 6
- cotangent: bfloat16 [8, 2048, 768], P('dp', 'seq'), may hold values from -6 to 6
- w_query: bfloat16 [768, 768], P(('dp', 'seq')), may hold values from -0.21875 to 0.21875
- w_key: bfloat16 [768, 768], P(('dp', 'seq')), may hold values from -0.21875 to 0.21875
- w_value: bfloat16 [768, 768], P(('dp', 'seq')), may hold values from -0.375 to 0.375
- w_output: bfloat16 [768, 768], P(('dp', 'seq')), may hold values from -0.375 to 0.375
- w_inner: bfloat16 [768, 3072], P(('dp', 'seq')), may hold values from -0.375 to 0.375
- w_outer: bfloat16 [3072, 768], P(('dp', 'seq')), may hold values from -0.1875 to 0.1875
- bias_query: bfloat16 [768], P(('dp', 'seq')), may hold values from -1.5 to 1.5
- bias_value: bfloat16 [768], P(('dp', 'seq')), may hold values from -1.5 to 1.5
- bias_output: bfloat16 [768], P(('dp', 'seq')), may hold values from -1.5 to 1.5
- bias_inner: bfloat16 [3072], P(('dp', 'seq')), may hold values from -1.5 to 1.5
- bias_outer: bfloat16 [768], P(('dp', 'seq')), may hold values from -1.5 to 1.5
- gain_input: bfloat16 [768], P(('dp', 'seq')), may hold values from 0.25 to 1.75
- bias_input: bfloat16 [768], P(('dp', 'seq')), may hold values from -1.5 to 1.5
- gain_attend: bfloat16 [768], P(('dp', 'seq')), may hold values from 0.25 to 1.75
- bias_attend: bfloat16 [768], P(('dp', 'seq')), may hold values from -1.5 to 1.5
- gain_middle: bfloat16 [768], P(('dp', 'seq')), may hold values from 0.25 to 1.75
- bias_middle: bfloat16 [768], P(('dp', 'seq')), may hold values from -1.5 to 1.5
- gain_hidden: bfloat16 [3072], P(('dp', 'seq')), may hold values from 0.25 to 1.75
- bias_hidden: bfloat16 [3072], P(('dp', 'seq')), may hold values from -1.5 to 1.5
Outputs:
- output: bfloat16 [8, 2048, 768], P('dp', 'seq')
- grad_tokens: float32 [8, 2048, 768], P('dp', 'seq')
- grad_w_query: float32 [768, 768], P(('dp', 'seq'))
- grad_w_key: float32 [768, 768], P(('dp', 'seq'))
- grad_w_value: float32 [768, 768], P(('dp', 'seq'))
- grad_w_output: float32 [768, 768], P(('dp', 'seq'))
- grad_w_inner: float32 [768, 3072], P(('dp', 'seq'))
- grad_w_outer: float32 [3072, 768], P(('dp', 'seq'))
- grad_bias_query: float32 [768], P(('dp', 'seq'))
- grad_bias_value: float32 [768], P(('dp', 'seq'))
- grad_bias_output: float32 [768], P(('dp', 'seq'))
- grad_bias_inner: float32 [3072], P(('dp', 'seq'))
- grad_bias_outer: float32 [768], P(('dp', 'seq'))
- grad_gain_input: float32 [768], P(('dp', 'seq'))
- grad_bias_input: float32 [768], P(('dp', 'seq'))
- grad_gain_attend: float32 [768], P(('dp', 'seq'))
- grad_bias_attend: float32 [768], P(('dp', 'seq'))
- grad_gain_middle: float32 [768], P(('dp', 'seq'))
- grad_bias_middle: float32 [768], P(('dp', 'seq'))
- grad_gain_hidden: float32 [3072], P(('dp', 'seq'))
- grad_bias_hidden: float32 [3072], P(('dp', 'seq'))
All inputs are finite; a program needn't handle non-finite values.
Results may differ from a plain program's by a relative error of at most 0.02.
Values may be sent and summed in bfloat16 or wider, within the bound.
No kernel may reach another device: no remote copies, remote signals or barrier semaphores. Data moves between devices by JAX's collectives and lax.ppermute only.
A program may use at most 192 MiB of HBM per device.

v0:
```python
import jax
import jax.numpy as jnp
from jax import lax
from jax.sharding import PartitionSpec as P

HEAD = 64
BLOCK = 256


EPSILON = 1e-05
MASKED = -1e30


def layer_norm(values, scaling, offset):
    centered = values - jnp.mean(values, axis=-1, keepdims=True)
    variance = jnp.mean(centered * centered, axis=-1, keepdims=True)
    return centered * lax.rsqrt(variance + EPSILON) * scaling + offset


def hidden_norm(hidden_pre, scaling, offset):
    return layer_norm(jax.nn.gelu(hidden_pre, approximate=False), scaling, offset)


def product(former, latter):
    return jnp.dot(former, latter, preferred_element_type=jnp.float32)


def product_left(former, latter):
    return jnp.einsum("ta,tb->ab", former, latter, preferred_element_type=jnp.float32)


def product_right(former, latter):
    return jnp.einsum("ta,ba->tb", former, latter, preferred_element_type=jnp.float32)


def column_sums(matrix):
    return jnp.sum(matrix.astype(jnp.float32), axis=0)


def head_pair(matrix, head_turn):
    pair_width = 2 * HEAD
    columns = lax.dynamic_slice_in_dim(matrix, head_turn * pair_width, pair_width, 2)
    return columns.reshape(matrix.shape[0], matrix.shape[1], 2, HEAD)


def place_pair(whole, part, head_turn):
    pair_width = 2 * HEAD
    flat_part = part.reshape(whole.shape[0], whole.shape[1], pair_width)
    return lax.dynamic_update_slice_in_dim(whole, flat_part, head_turn * pair_width, 2)


def stat_pair(stats, head_turn):
    picked = lax.dynamic_slice_in_dim(stats, head_turn * 2, 2, 2)
    return jnp.transpose(picked, (0, 2, 1))[..., None]


def place_stat(stats, values, head_turn):
    return lax.dynamic_update_slice_in_dim(
        stats, jnp.transpose(values[..., 0], (0, 2, 1)), head_turn * 2, 2
    )


def pair_scores(query_pair, key_pair, visible):
    scores = jnp.einsum(
        "gqhd,gkhd->ghqk", query_pair, key_pair, preferred_element_type=jnp.float32
    ) * HEAD ** (-0.5)
    return jnp.where(visible[None, None, :, :], scores, MASKED)


def attend_forward(queries, keys_all, values_all, visible):
    groups, row_count, width = queries.shape

    def head_body(head_turn, carried):
        attended, logsum = carried
        masked = pair_scores(head_pair(queries, head_turn), head_pair(keys_all, head_turn), visible)
        largest = jnp.max(masked, axis=-1, keepdims=True)
        powered = jnp.exp(masked - largest)
        totals = jnp.sum(powered, axis=-1, keepdims=True)
        shares = (powered / totals).astype(jnp.bfloat16)
        mixture = jnp.einsum(
            "ghqk,gkhd->gqhd",
            shares,
            head_pair(values_all, head_turn),
            preferred_element_type=jnp.float32,
        )
        attended = place_pair(attended, mixture, head_turn)
        logsum = place_stat(logsum, largest + jnp.log(totals), head_turn)
        return (attended, logsum)

    initial = (
        jnp.zeros((groups, row_count, width), jnp.float32),
        jnp.zeros((groups, row_count, width // HEAD), jnp.float32),
    )
    return lax.fori_loop(0, width // (2 * HEAD), head_body, initial)


def attend_backward(queries, keys_all, values_all, grad_attended, logsum, visible):
    groups, row_count, width = queries.shape
    key_count = keys_all.shape[1]

    def head_body(head_turn, carried):
        query_pair = head_pair(queries, head_turn)
        key_pair = head_pair(keys_all, head_turn)
        grad_pair = head_pair(grad_attended, head_turn)
        masked = pair_scores(query_pair, key_pair, visible)
        shares = jnp.exp(masked - stat_pair(logsum, head_turn))
        grad_shares = jnp.einsum(
            "gqhd,gkhd->ghqk",
            grad_pair,
            head_pair(values_all, head_turn),
            preferred_element_type=jnp.float32,
        )
        row_inner = jnp.sum(shares * grad_shares, axis=-1, keepdims=True)
        grad_scores = (shares * (grad_shares - row_inner)).astype(jnp.bfloat16)
        query_part = jnp.einsum(
            "ghqk,gkhd->gqhd", grad_scores, key_pair, preferred_element_type=jnp.float32
        ) * HEAD ** (-0.5)
        updated = (
            place_pair(carried[0], query_part, head_turn),
            place_stat(carried[1], row_inner, head_turn),
        )
        key_part = jnp.einsum(
            "ghqk,gqhd->gkhd", grad_scores, query_pair, preferred_element_type=jnp.float32
        ) * HEAD ** (-0.5)
        value_part = jnp.einsum(
            "ghqk,gqhd->gkhd",
            shares.astype(jnp.bfloat16),
            grad_pair,
            preferred_element_type=jnp.float32,
        )
        updated = updated + (
            place_pair(carried[2], key_part, head_turn),
            place_pair(carried[3], value_part, head_turn),
        )
        return updated

    initial = (
        jnp.zeros((groups, row_count, width), jnp.float32),
        jnp.zeros((groups, row_count, width // HEAD), jnp.float32),
    )
    initial = initial + (
        jnp.zeros((groups, key_count, width), jnp.float32),
        jnp.zeros((groups, key_count, width), jnp.float32),
    )
    return lax.fori_loop(0, width // (2 * HEAD), head_body, initial)


def vector_params(gathered):
    return tuple((member.astype(jnp.float32) for member in gathered[6:]))


def per_device(
    tokens,
    cotangent,
    w_query,
    w_key,
    w_value,
    w_output,
    w_inner,
    w_outer,
    bias_query,
    bias_value,
    bias_output,
    bias_inner,
    bias_outer,
    gain_input,
    bias_input,
    gain_attend,
    bias_attend,
    gain_middle,
    bias_middle,
    gain_hidden,
    bias_hidden,
):
    gathered = (
        lax.all_gather(w_query, ("dp", "seq"), axis=0, tiled=True),
        lax.all_gather(w_key, ("dp", "seq"), axis=0, tiled=True),
        lax.all_gather(w_value, ("dp", "seq"), axis=0, tiled=True),
        lax.all_gather(w_output, ("dp", "seq"), axis=0, tiled=True),
        lax.all_gather(w_inner, ("dp", "seq"), axis=0, tiled=True),
        lax.all_gather(w_outer, ("dp", "seq"), axis=0, tiled=True),
        lax.all_gather(bias_query, ("dp", "seq"), axis=0, tiled=True),
        lax.all_gather(bias_value, ("dp", "seq"), axis=0, tiled=True),
        lax.all_gather(bias_output, ("dp", "seq"), axis=0, tiled=True),
        lax.all_gather(bias_inner, ("dp", "seq"), axis=0, tiled=True),
        lax.all_gather(bias_outer, ("dp", "seq"), axis=0, tiled=True),
        lax.all_gather(gain_input, ("dp", "seq"), axis=0, tiled=True),
        lax.all_gather(bias_input, ("dp", "seq"), axis=0, tiled=True),
        lax.all_gather(gain_attend, ("dp", "seq"), axis=0, tiled=True),
        lax.all_gather(bias_attend, ("dp", "seq"), axis=0, tiled=True),
        lax.all_gather(gain_middle, ("dp", "seq"), axis=0, tiled=True),
        lax.all_gather(bias_middle, ("dp", "seq"), axis=0, tiled=True),
        lax.all_gather(gain_hidden, ("dp", "seq"), axis=0, tiled=True),
        lax.all_gather(bias_hidden, ("dp", "seq"), axis=0, tiled=True),
    )
    query_full, key_full, value_full, output_full, inner_full, outer_full = gathered[:6]
    (
        bq_full,
        bv_full,
        bo_full,
        bi_full,
        bu_full,
        gin_full,
        bin_full,
        gat_full,
        bat_full,
        gmi_full,
        bmi_full,
        ghi_full,
        bhi_full,
    ) = vector_params(gathered)
    groups, row_count, width = tokens.shape
    flat_rows = groups * row_count
    seq_place = lax.axis_index("seq")
    own_pos = seq_place * row_count + jnp.arange(row_count, dtype=jnp.int32)
    all_pos = jnp.arange(row_count * lax.axis_size("seq"), dtype=jnp.int32)
    visible = all_pos[None, :] // BLOCK <= own_pos[:, None] // BLOCK
    inputs = tokens.astype(jnp.float32).reshape(flat_rows, width)
    normed_low = layer_norm(inputs, gin_full, bin_full).astype(jnp.bfloat16)
    queries = (
        (product(normed_low, query_full) + bq_full)
        .astype(jnp.bfloat16)
        .reshape(groups, row_count, width)
    )
    keys_own = product(normed_low, key_full).astype(jnp.bfloat16).reshape(groups, row_count, width)
    values_own = (
        (product(normed_low, value_full) + bv_full)
        .astype(jnp.bfloat16)
        .reshape(groups, row_count, width)
    )
    keys_all, values_all = (
        lax.all_gather(keys_own, "seq", axis=1, tiled=True),
        lax.all_gather(values_own, "seq", axis=1, tiled=True),
    )
    attended, logsum = attend_forward(queries, keys_all, values_all, visible)
    attended = attended.reshape(flat_rows, width)
    sub_low = layer_norm(attended, gat_full, bat_full).astype(jnp.bfloat16)
    middle = inputs + product(sub_low, output_full) + bo_full
    normed_mid = layer_norm(middle, gmi_full, bmi_full).astype(jnp.bfloat16)
    hidden_pre = product(normed_mid, inner_full) + bi_full
    hidden_low = hidden_norm(hidden_pre, ghi_full, bhi_full).astype(jnp.bfloat16)
    output = (middle + product(hidden_low, outer_full) + bu_full).astype(jnp.bfloat16)
    regathered = (
        lax.all_gather(w_query, ("dp", "seq"), axis=0, tiled=True),
        lax.all_gather(w_key, ("dp", "seq"), axis=0, tiled=True),
        lax.all_gather(w_value, ("dp", "seq"), axis=0, tiled=True),
        lax.all_gather(w_output, ("dp", "seq"), axis=0, tiled=True),
        lax.all_gather(w_inner, ("dp", "seq"), axis=0, tiled=True),
        lax.all_gather(w_outer, ("dp", "seq"), axis=0, tiled=True),
        lax.all_gather(bias_query, ("dp", "seq"), axis=0, tiled=True),
        lax.all_gather(bias_value, ("dp", "seq"), axis=0, tiled=True),
        lax.all_gather(bias_output, ("dp", "seq"), axis=0, tiled=True),
        lax.all_gather(bias_inner, ("dp", "seq"), axis=0, tiled=True),
        lax.all_gather(bias_outer, ("dp", "seq"), axis=0, tiled=True),
        lax.all_gather(gain_input, ("dp", "seq"), axis=0, tiled=True),
        lax.all_gather(bias_input, ("dp", "seq"), axis=0, tiled=True),
        lax.all_gather(gain_attend, ("dp", "seq"), axis=0, tiled=True),
        lax.all_gather(bias_attend, ("dp", "seq"), axis=0, tiled=True),
        lax.all_gather(gain_middle, ("dp", "seq"), axis=0, tiled=True),
        lax.all_gather(bias_middle, ("dp", "seq"), axis=0, tiled=True),
        lax.all_gather(gain_hidden, ("dp", "seq"), axis=0, tiled=True),
        lax.all_gather(bias_hidden, ("dp", "seq"), axis=0, tiled=True),
    )
    keys_back, values_back = (
        lax.all_gather(keys_own, "seq", axis=1, tiled=True),
        lax.all_gather(values_own, "seq", axis=1, tiled=True),
    )
    query_back, key_back, value_back, output_back, inner_back, outer_back = regathered[:6]
    (
        bq_back,
        bv_back,
        bo_back,
        bi_back,
        bu_back,
        gin_back,
        bin_back,
        gat_back,
        bat_back,
        gmi_back,
        bmi_back,
        ghi_back,
        bhi_back,
    ) = vector_params(regathered)
    cotangent_flat = cotangent.reshape(flat_rows, width)
    grad_output = cotangent_flat.astype(jnp.float32)
    grad_w_outer = product_left(hidden_low, cotangent_flat)
    grad_bias_outer = column_sums(cotangent_flat)
    grad_hidden = product_right(cotangent_flat, outer_back)
    unused, pull_hidden = jax.vjp(hidden_norm, hidden_pre, ghi_back, bhi_back)
    grad_pre, grad_gain_hidden, grad_bias_hidden = pull_hidden(grad_hidden)
    grad_pre_low = grad_pre.astype(jnp.bfloat16)
    grad_w_inner = product_left(normed_mid, grad_pre_low)
    grad_bias_inner = column_sums(grad_pre_low)
    grad_normed_mid = product_right(grad_pre_low, inner_back)
    unused, pull_middle = jax.vjp(layer_norm, middle, gmi_back, bmi_back)
    grad_mid_part, grad_gain_middle, grad_bias_middle = pull_middle(grad_normed_mid)
    grad_middle = grad_output + grad_mid_part
    grad_branch = grad_middle.astype(jnp.bfloat16)
    grad_w_output = product_left(sub_low, grad_branch)
    grad_bias_output = column_sums(grad_branch)
    grad_sub = product_right(grad_branch, output_back)
    unused, pull_attend = jax.vjp(layer_norm, attended, gat_back, bat_back)
    grad_att, grad_gain_attend, grad_bias_attend = pull_attend(grad_sub)
    grad_attended = grad_att.astype(jnp.bfloat16).reshape(groups, row_count, width)
    grad_query, row_inner, key_part, value_part = attend_backward(
        queries, keys_back, values_back, grad_attended, logsum, visible
    )
    key_sum, value_sum = (
        lax.psum_scatter(
            key_part.astype(jnp.bfloat16), "seq", scatter_dimension=1, tiled=True
        ).astype(jnp.float32),
        lax.psum_scatter(
            value_part.astype(jnp.bfloat16), "seq", scatter_dimension=1, tiled=True
        ).astype(jnp.float32),
    )
    grad_query_low = grad_query.astype(jnp.bfloat16).reshape(flat_rows, width)
    grad_key_low = key_sum.astype(jnp.bfloat16).reshape(flat_rows, width)
    grad_value_low = value_sum.astype(jnp.bfloat16).reshape(flat_rows, width)
    grad_w_query = product_left(normed_low, grad_query_low)
    grad_bias_query = column_sums(grad_query_low)
    grad_w_key = product_left(normed_low, grad_key_low)
    grad_w_value = product_left(normed_low, grad_value_low)
    grad_bias_value = column_sums(grad_value_low)
    grad_normed = (
        product_right(grad_query_low, query_back)
        + product_right(grad_key_low, key_back)
        + product_right(grad_value_low, value_back)
    )
    unused, pull_input = jax.vjp(layer_norm, inputs, gin_back, bin_back)
    grad_in_part, grad_gain_input, grad_bias_input = pull_input(grad_normed)
    grad_tokens = (grad_middle + grad_in_part).reshape(groups, row_count, width)
    owned = (
        lax.psum_scatter(grad_w_query, ("dp", "seq"), scatter_dimension=0, tiled=True),
        lax.psum_scatter(grad_w_key, ("dp", "seq"), scatter_dimension=0, tiled=True),
        lax.psum_scatter(grad_w_value, ("dp", "seq"), scatter_dimension=0, tiled=True),
        lax.psum_scatter(grad_w_output, ("dp", "seq"), scatter_dimension=0, tiled=True),
        lax.psum_scatter(grad_w_inner, ("dp", "seq"), scatter_dimension=0, tiled=True),
        lax.psum_scatter(grad_w_outer, ("dp", "seq"), scatter_dimension=0, tiled=True),
        lax.psum_scatter(grad_bias_query, ("dp", "seq"), scatter_dimension=0, tiled=True),
        lax.psum_scatter(grad_bias_value, ("dp", "seq"), scatter_dimension=0, tiled=True),
        lax.psum_scatter(grad_bias_output, ("dp", "seq"), scatter_dimension=0, tiled=True),
        lax.psum_scatter(grad_bias_inner, ("dp", "seq"), scatter_dimension=0, tiled=True),
        lax.psum_scatter(grad_bias_outer, ("dp", "seq"), scatter_dimension=0, tiled=True),
        lax.psum_scatter(grad_gain_input, ("dp", "seq"), scatter_dimension=0, tiled=True),
        lax.psum_scatter(grad_bias_input, ("dp", "seq"), scatter_dimension=0, tiled=True),
        lax.psum_scatter(grad_gain_attend, ("dp", "seq"), scatter_dimension=0, tiled=True),
        lax.psum_scatter(grad_bias_attend, ("dp", "seq"), scatter_dimension=0, tiled=True),
        lax.psum_scatter(grad_gain_middle, ("dp", "seq"), scatter_dimension=0, tiled=True),
        lax.psum_scatter(grad_bias_middle, ("dp", "seq"), scatter_dimension=0, tiled=True),
        lax.psum_scatter(grad_gain_hidden, ("dp", "seq"), scatter_dimension=0, tiled=True),
        lax.psum_scatter(grad_bias_hidden, ("dp", "seq"), scatter_dimension=0, tiled=True),
    )
    return (
        output.reshape(groups, row_count, width),
        grad_tokens,
        owned[0],
        owned[1],
        owned[2],
        owned[3],
        owned[4],
        owned[5],
        owned[6],
        owned[7],
        owned[8],
        owned[9],
        owned[10],
        owned[11],
        owned[12],
        owned[13],
        owned[14],
        owned[15],
        owned[16],
        owned[17],
        owned[18],
    )


def solution(mesh):
    return jax.shard_map(
        per_device,
        mesh=mesh,
        in_specs=(
            P("dp", "seq", None),
            P("dp", "seq", None),
            P(("dp", "seq"), None),
            P(("dp", "seq"), None),
            P(("dp", "seq"), None),
            P(("dp", "seq"), None),
            P(("dp", "seq"), None),
            P(("dp", "seq"), None),
            P(("dp", "seq")),
            P(("dp", "seq")),
            P(("dp", "seq")),
            P(("dp", "seq")),
            P(("dp", "seq")),
            P(("dp", "seq")),
            P(("dp", "seq")),
            P(("dp", "seq")),
            P(("dp", "seq")),
            P(("dp", "seq")),
            P(("dp", "seq")),
            P(("dp", "seq")),
            P(("dp", "seq")),
        ),
        out_specs=(
            P("dp", "seq", None),
            P("dp", "seq", None),
            P(("dp", "seq"), None),
            P(("dp", "seq"), None),
            P(("dp", "seq"), None),
            P(("dp", "seq"), None),
            P(("dp", "seq"), None),
            P(("dp", "seq"), None),
            P(("dp", "seq")),
            P(("dp", "seq")),
            P(("dp", "seq")),
            P(("dp", "seq")),
            P(("dp", "seq")),
            P(("dp", "seq")),
            P(("dp", "seq")),
            P(("dp", "seq")),
            P(("dp", "seq")),
            P(("dp", "seq")),
            P(("dp", "seq")),
            P(("dp", "seq")),
            P(("dp", "seq")),
        ),
        check_vma=False,
    )
```

profile of v0, /device:TPU:0, one launch (start us, length us, event | category | flops | bytes accessed | tf_op | source)
XLA Modules:
  0.0 1667.1 jit_solution(7981153631746962493)
XLA Ops:
  20.4 42.9 %all-reduce.27 = (bf16[768]{0:T(1024)(128)(2,1)S(1)}, bf16[768]{0:T(1024)(128)(2,1)S(1)}, bf16[768]{0:T(1024)(128)(2,1)S(1)}, bf16[768]{0:T(1024)(128)(2,1)S(1)}...) all-reduce(bf16[768]{0:T(1024)(128)(2,1)S(1)} %dynamic-update-slice, ...), channel_id=1, replica_groups=mesh['dp'=8,'seq'=4] {'dp','seq'}, use_global_device_ids=true, to_apply=%add.6 | all-reduce | flops 16896 | bytes 67584
  67.8 3.3 add_convert_fusion.7
  71.2 52.4 %all-gather.15.cloned.1.call-done = bf16[768,768]{1,0:T(8,128)(2,1)} async-done(((bf16[24,768]{1,0:T(8,128)(2,1)}), bf16[768,768]{1,0:T(8,128)(2,1)}) %all-gather.15.cloned.1.call-update) | async-done | bytes 1179664 | tf_op jit(solution)/shard_map/all_gather | solution.py:177
  123.6 3.1 convolution_convert_fusion
  130.7 48.8 %all-gather.13.cloned.1.call-done = bf16[768,768]{1,0:T(8,128)(2,1)} async-done(((bf16[24,768]{1,0:T(8,128)(2,1)}), bf16[768,768]{1,0:T(8,128)(2,1)}) %all-gather.13.cloned.1.call-update) | async-done | bytes 1179664 | tf_op jit(solution)/shard_map/all_gather | solution.py:176
  181.9 62.0 %all-gather.23.cloned.1.call-done = bf16[2048,768]{1,0:T(8,128)(2,1)} async-done(((bf16[512,768]{1,0:T(8,128)(2,1)}), bf16[2048,768]{1,0:T(8,128)(2,1)}) %all-gather.23.cloned.1.call-update) | async-done | bytes 3145744 | tf_op jit(solution)/shard_map/all_gather | solution.py:233
  243.9 4.7 copy.50
  248.7 59.4 %all-gather.25.cloned.1.call-done = bf16[2048,768]{1,0:T(8,128)(2,1)} async-done(((bf16[512,768]{1,0:T(8,128)(2,1)}), bf16[2048,768]{1,0:T(8,128)(2,1)}) %all-gather.25.cloned.1.call-update) | async-done | bytes 3145744 | tf_op jit(solution)/shard_map/all_gather | solution.py:232
  308.1 4.7 copy.52
  313.0 55.2 %while.34 = (s32[]{:T(128)}, f32[1,512,768]{1,2,0:T(8,128)S(1)}, f32[1,512,12]{1,2,0:T(8,128)S(1)}, bf16[1,2048,768]{1,2,0:T(8,128)(2,1)}, bf16[1,512,768]{1,2,0...) while((s32[]{:T(128)}, f32[1,512,768]{1,2,0:T(8,128)S(1)}, ...), condition=%wide.region_5.6_spmd.clone, body=%wide.region_2.5_spmd.clone.sunk | while | flops 563084288 | bytes 33728760 | solution.py:94
  317.0 2.5 fusion.142
  319.5 2.6 fusion.143
  326.2 2.5 fusion.142
  328.7 2.6 fusion.143
  335.4 2.5 fusion.142
  337.9 2.6 fusion.143
  347.1 2.6 fusion.143
  356.3 2.6 fusion.143
  363.0 2.5 fusion.142
  365.5 2.6 fusion.143
  377.0 51.9 %all-gather.19.cloned.1.call-done = bf16[768,3072]{1,0:T(8,128)(2,1)} async-done(((bf16[24,3072]{1,0:T(8,128)(2,1)}), bf16[768,3072]{1,0:T(8,128)(2,1)}) %all-gather.19.cloned.1.call-update) | async-done | bytes 4718608 | tf_op jit(solution)/shard_map/all_gather | solution.py:180
  428.9 21.8 %fusion.86 = (f32[512]{0:T(512)S(1)}, f32[512,3072]{1,0:T(8,128)}, f32[512,3072]{1,0:T(8,128)}, f32[512,3072]{1,0:T(8,128)}) fusion(f32[3072]{0:T(1024)S(1)} %convert_element_type.155, bf16[768,3072]{1,0:T(8,128)(2,1)} %all-gather.19.cloned.1.call-done, f32[512,768]{1,0:T(8,128)} %copy-done.5, f32[768]{0:T(1024)S(1)} %convert_element_type.153, ...), kind=kOutput, calls=%fused_computation.169 | convolution fusion | flops 2521693696 | bytes 25190400 | tf_op jit(solution)/shard_map/dot_general | solution.py:25
  450.7 43.4 %all-gather.21.cloned.1.call-done = bf16[3072,768]{1,0:T(8,128)(2,1)} async-done(((bf16[96,768]{1,0:T(8,128)(2,1)}), bf16[3072,768]{1,0:T(8,128)(2,1)}) %all-gather.21.cloned.1.call-update) | async-done | bytes 4718608 | tf_op jit(solution)/shard_map/all_gather | solution.py:181
  494.1 7.4 multiply_reduce_fusion.2
  501.5 3.3 multiply_reduce_fusion.1
  504.9 11.1 convert_reduce_fusion
  516.0 7.1 multiply_reduce_fusion.4
  532.4 142.4 %while.35 = (s32[]{:T(128)}, bf16[1,512,768]{1,2,0:T(8,128)(2,1)}, bf16[1,2048,768]{1,2,0:T(8,128)(2,1)}, bf16[1,2048,768]{1,2,0:T(8,128)(2,1)}, bf16[1,2048,768...) while((s32[]{:T(128)}, bf16[1,512,768]{1,2,0:T(8,128)(2,1)}, ...), condition=%wide.region_20.21_spmd.clone, body=%wide.region_18.20_spmd.clone.sunk | while | flops 1375337472 | bytes 107321784 | solution.py:145
  533.8 4.5 fusion.154
  541.2 5.6 multiply_reduce_fusion.11
  547.1 2.5 multiply_convert_fusion.2
  557.5 4.5 fusion.154
  564.9 5.6 multiply_reduce_fusion.11
  570.8 2.5 multiply_convert_fusion.2
  581.3 4.5 fusion.154
  588.6 5.6 multiply_reduce_fusion.11
  594.5 2.5 multiply_convert_fusion.2
  605.0 4.5 fusion.154
  612.4 5.6 multiply_reduce_fusion.11
  618.3 2.5 multiply_convert_fusion.2
  628.7 4.5 fusion.154
  636.1 5.6 multiply_reduce_fusion.11
  642.0 2.5 multiply_convert_fusion.2
  652.5 4.5 fusion.154
  659.8 5.6 multiply_reduce_fusion.11
  665.7 2.5 multiply_convert_fusion.2
  676.7 3.3 fusion.54
  680.0 54.0 %reduce-scatter.9.cloned.1.call-done = bf16[1,512,768]{1,2,0:T(8,128)(2,1)} async-done(((bf16[1,2048,768]{1,2,0:T(8,128)(2,1)}), bf16[1,512,768]{1,2,0:T(8,128)(2,1)}) %reduce-scatter.9.cloned.1.call-update) | async-done | bytes 786448 | tf_op jit(solution)/shard_map/reduce_scatter | solution.py:309
  734.0 3.5 fusion.50
  737.5 59.0 %reduce-scatter.11.cloned.1.call-done = bf16[1,512,768]{1,2,0:T(8,128)(2,1)} async-done(((bf16[1,2048,768]{1,2,0:T(8,128)(2,1)}), bf16[1,512,768]{1,2,0:T(8,128)(2,1)}) %reduce-scatter.11.cloned.1.call-update) | async-done | bytes 786448 | tf_op jit(solution)/shard_map/reduce_scatter | solution.py:312
  796.5 4.4 fusion.82
  805.7 2.5 fusion.52
  808.3 3.5 fusion.73
  811.9 3.7 fusion.48
  818.3 7.2 fusion.74
  826.7 8.2 fusion.56
  835.6 6.8 fusion.41
  842.3 111.7 %all-reduce.30.cloned.1.call-done = (f32[768]{0:T(1024)}, f32[768]{0:T(1024)}, f32[768]{0:T(1024)}, f32[3072]{0:T(1024)}, f32[768]{0:T(1024)}, /*index=5*/f32[76...) async-done(((f32[768]{0:T(1024)}, f32[768]{0:T(1024)}, f32[768]{0:T(1024)}, ...) | async-done | bytes 67600
  970.5 93.6 %reduce-scatter.13.cloned.1.call-done = f32[24,768]{1,0:T(8,128)} async-done(((f32[768,768]{1,0:T(8,128)}), f32[24,768]{1,0:T(8,128)}) %reduce-scatter.13.cloned.1.call-update) | async-done | bytes 73744 | tf_op jit(solution)/shard_map/reduce_scatter | solution.py:333
  1064.0 104.8 %reduce-scatter.19.cloned.1.call-done = f32[24,768]{1,0:T(8,128)} async-done(((f32[768,768]{1,0:T(8,128)}), f32[24,768]{1,0:T(8,128)}) %reduce-scatter.19.cloned.1.call-update) | async-done | bytes 73744 | tf_op jit(solution)/shard_map/reduce_scatter | solution.py:336
  1168.8 103.8 %reduce-scatter.15.cloned.1.call-done = f32[24,768]{1,0:T(8,128)} async-done(((f32[768,768]{1,0:T(8,128)}), f32[24,768]{1,0:T(8,128)}) %reduce-scatter.15.cloned.1.call-update) | async-done | bytes 73744 | tf_op jit(solution)/shard_map/reduce_scatter | solution.py:334
  1272.6 104.6 %reduce-scatter.17.cloned.1.call-done = f32[24,768]{1,0:T(8,128)} async-done(((f32[768,768]{1,0:T(8,128)}), f32[24,768]{1,0:T(8,128)}) %reduce-scatter.17.cloned.1.call-update) | async-done | bytes 73744 | tf_op jit(solution)/shard_map/reduce_scatter | solution.py:335
  1377.2 141.0 %reduce-scatter.21.cloned.1.call-done = f32[24,3072]{1,0:T(8,128)} async-done(((f32[768,3072]{1,0:T(8,128)}), f32[24,3072]{1,0:T(8,128)}) %reduce-scatter.21.cloned.1.call-update) | async-done | bytes 294928 | tf_op jit(solution)/shard_map/reduce_scatter | solution.py:337
  1518.2 141.9 %reduce-scatter.23.cloned.1.call-done = f32[96,768]{1,0:T(8,128)} async-done(((f32[3072,768]{1,0:T(8,128)}), f32[96,768]{1,0:T(8,128)}) %reduce-scatter.23.cloned.1.call-update) | async-done | bytes 294928 | tf_op jit(solution)/shard_map/reduce_scatter | solution.py:338
  (416 shorter events, 164.1 us)
Async XLA Ops:
  7.2 60.6 %all-gather.11.cloned.1.call-start = ((), (), s32[]{:S(2)}) async-start(), calls=%async_computation.8 | async-start | bytes 1216512 | tf_op jit(solution)/shard_map/all_gather | solution.py:178
  7.9 115.6 %all-gather.15.cloned.1.call-start = ((), (), s32[]{:S(2)}) async-start(), calls=%async_computation.10 | async-start | bytes 1216512 | tf_op jit(solution)/shard_map/all_gather | solution.py:177
  8.7 170.8 %all-gather.13.cloned.1.call-start = ((), (), s32[]{:S(2)}) async-start(), calls=%async_computation.9 | async-start | bytes 1216512 | tf_op jit(solution)/shard_map/all_gather | solution.py:176
  9.4 234.5 %all-gather.23.cloned.1.call-start = ((), (), s32[]{:S(2)}) async-start(), calls=%async_computation.22 | async-start | bytes 3932160 | tf_op jit(solution)/shard_map/all_gather | solution.py:233
  63.3 116.1 %copy-start.43 = (f32[768]{0:T(1024)}, f32[768]{0:T(1024)S(1)}, u32[]{:S(2)}) copy-start(f32[768]{0:T(1024)S(1)} %convert_element_type.141) | copy-start | bytes 9220
  63.3 116.1 %copy-start.20 = (f32[768]{0:T(1024)}, f32[768]{0:T(1024)S(1)}, u32[]{:S(2)}) copy-start(f32[768]{0:T(1024)S(1)} %convert_element_type.140) | copy-start | bytes 9220
  64.7 114.8 %copy-start.22 = (f32[512]{0:T(512)}, f32[512]{0:T(512)S(1)}, u32[]{:S(2)}) copy-start(f32[512]{0:T(512)S(1)} %broadcast_multiply_fusion.3) | copy-start | bytes 6148
  66.8 112.7 %copy-start.25 = (f32[512]{0:T(512)}, f32[512]{0:T(512)S(1)}, u32[]{:S(2)}) copy-start(f32[512]{0:T(512)S(1)} %fusion.66) | copy-start | bytes 6148
  66.8 56.8 %copy-start = (bf16[1,512,768]{2,1,0:T(8,128)(2,1)S(1)}, bf16[1,512,768]{2,1,0:T(8,128)(2,1)}, u32[]{:S(2)}) copy-start(bf16[1,512,768]{2,1,0:T(8,128)(2,1)} %param.25) | copy-start | bytes 2359300
  71.2 236.9 %all-gather.25.cloned.1.call-start = ((), (), s32[]{:S(2)}) async-start(), calls=%async_computation.23 | async-start | bytes 3932160 | tf_op jit(solution)/shard_map/all_gather | solution.py:232
  126.7 246.5 %all-gather.17.cloned.1.call-start = ((), (), s32[]{:S(2)}) async-start(), calls=%async_computation.11 | async-start | bytes 1216512 | tf_op jit(solution)/shard_map/all_gather | solution.py:179
  127.2 301.7 %all-gather.19.cloned.1.call-start = ((), (), s32[]{:S(2)}) async-start(), calls=%async_computation.12 | async-start | bytes 4866048 | tf_op jit(solution)/shard_map/all_gather | solution.py:180
  128.0 366.1 %all-gather.21.cloned.1.call-start = ((), (), s32[]{:S(2)}) async-start(), calls=%async_computation.13 | async-start | bytes 4866048 | tf_op jit(solution)/shard_map/all_gather | solution.py:181
  128.7 605.3 %reduce-scatter.9.cloned.1.call-start = ((), (), s32[]{:S(2)}) async-start(), calls=%async_computation.14 | async-start | bytes 3932160 | tf_op jit(solution)/shard_map/reduce_scatter | solution.py:309
  130.0 243.2 %copy-start.47 = (f32[768]{0:T(1024)}, f32[768]{0:T(1024)S(1)}, u32[]{:S(2)}) copy-start(f32[768]{0:T(1024)S(1)} %convert_element_type.149) | copy-start | bytes 9220
  130.0 396.6 %copy-start.37 = (f32[768]{0:T(1024)}, f32[768]{0:T(1024)S(1)}, u32[]{:S(2)}) copy-start(f32[768]{0:T(1024)S(1)} %convert_element_type.148) | copy-start | bytes 9220
  130.0 298.9 %copy-start.45 = (f32[768]{0:T(1024)}, f32[768]{0:T(1024)S(1)}, u32[]{:S(2)}) copy-start(f32[768]{0:T(1024)S(1)} %convert_element_type.153) | copy-start | bytes 9220
  130.0 393.0 %copy-start.35 = (f32[768]{0:T(1024)}, f32[768]{0:T(1024)S(1)}, u32[]{:S(2)}) copy-start(f32[768]{0:T(1024)S(1)} %convert_element_type.152) | copy-start | bytes 9220
  372.8 153.7 %copy-start.29 = (f32[512]{0:T(512)}, f32[512]{0:T(512)S(1)}, u32[]{:S(2)}) copy-start(f32[512]{0:T(512)S(1)} %broadcast_multiply_fusion.2) | copy-start | bytes 6148
  373.1 153.4 %copy-start.41 = (f32[512]{0:T(512)}, f32[512]{0:T(512)S(1)}, u32[]{:S(2)}) copy-start(f32[512]{0:T(512)S(1)} %fusion.67) | copy-start | bytes 6148
  375.5 147.6 %copy-start.27 = (f32[512]{0:T(512)}, f32[512]{0:T(512)S(1)}, u32[]{:S(2)}) copy-start(f32[512]{0:T(512)S(1)} %broadcast_multiply_fusion.1) | copy-start | bytes 6148
  377.0 146.1 %copy-start.39 = (f32[512]{0:T(512)}, f32[512]{0:T(512)S(1)}, u32[]{:S(2)}) copy-start(f32[512]{0:T(512)S(1)} %fusion.68) | copy-start | bytes 6148
  377.0 117.2 %copy-start.14 = (bf16[1,512,768]{2,1,0:T(8,128)(2,1)S(1)}, bf16[1,512,768]{2,1,0:T(8,128)(2,1)}, u32[]{:S(2)}) copy-start(bf16[1,512,768]{2,1,0:T(8,128)(2,1)} %param.26) | copy-start | bytes 2359300
  494.1 7.4 slice-start.2
  494.1 7.4 slice-start.3
  504.9 11.1 copy-start.6
  515.9 7.1 copy-start.10
  532.4 5.9 copy-start.8
  532.4 5.9 copy-start.18
  541.1 5.7 slice-start
  541.1 5.9 slice-start.1
  556.1 6.0 copy-start.8
  556.1 6.0 copy-start.18
  564.9 5.7 slice-start
  564.9 5.9 slice-start.1
  579.8 6.0 copy-start.8
  579.8 6.0 copy-start.18
  588.6 5.9 slice-start.1
  603.6 6.0 copy-start.8
  603.6 6.0 copy-start.18
  612.3 5.9 slice-start.1
  627.3 5.9 copy-start.8
  627.3 5.9 copy-start.18
  636.0 5.7 slice-start
  636.1 5.9 slice-start.1
  651.0 5.9 copy-start.8
  651.0 5.9 copy-start.18
  659.8 5.9 slice-start.1
  674.8 121.7 %reduce-scatter.11.cloned.1.call-start = ((), (), s32[]{:S(2)}) async-start(), calls=%async_computation.15 | async-start | bytes 3932160 | tf_op jit(solution)/shard_map/reduce_scatter | solution.py:312
  675.4 278.6 %all-reduce.30.cloned.1.call-start = ((), (), s32[]{:S(2)}) async-start(), calls=%async_computation.24 | async-start | bytes 155648
  676.7 119.8 %copy-start.1 = (bf16[1,512,768]{2,1,0:T(8,128)(2,1)S(1)}, bf16[1,512,768]{2,1,0:T(8,128)(2,1)}, u32[]{:S(2)}) copy-start(bf16[1,512,768]{2,1,0:T(8,128)(2,1)} %param.25) | copy-start | bytes 2359300
  676.7 119.8 %copy-start.21 = (f32[768]{0:T(1024)S(1)}, f32[768]{0:T(1024)}, u32[]{:S(2)}) copy-start(f32[768]{0:T(1024)} %copy-done.20) | copy-start | bytes 9220
  676.7 119.8 %copy-start.23 = (f32[512]{0:T(512)S(1)}, f32[512]{0:T(512)}, u32[]{:S(2)}) copy-start(f32[512]{0:T(512)} %copy-done.22) | copy-start | bytes 6148
  737.5 63.4 %copy-start.32 = (f32[512]{0:T(512)S(1)}, f32[512]{0:T(512)}, u32[]{:S(2)}) copy-start(f32[512]{0:T(512)} %copy-done.31) | copy-start | bytes 6148
  737.5 63.4 %copy-start.26 = (f32[512]{0:T(512)S(1)}, f32[512]{0:T(512)}, u32[]{:S(2)}) copy-start(f32[512]{0:T(512)} %copy-done.25) | copy-start | bytes 6148
  737.5 64.8 %copy-start.34 = (f32[512]{0:T(512)S(1)}, f32[512]{0:T(512)}, u32[]{:S(2)}) copy-start(f32[512]{0:T(512)} %copy-done.33) | copy-start | bytes 6148
  796.5 5.8 copy-start.4
  796.5 5.8 copy-start.15
  805.6 258.4 %reduce-scatter.13.cloned.1.call-start = ((), (), s32[]{:S(2)}) async-start(), calls=%async_computation.16 | async-start | bytes 2433024 | tf_op jit(solution)/shard_map/reduce_scatter | solution.py:333
  808.2 360.6 %reduce-scatter.19.cloned.1.call-start = ((), (), s32[]{:S(2)}) async-start(), calls=%async_computation.19 | async-start | bytes 2433024 | tf_op jit(solution)/shard_map/reduce_scatter | solution.py:336
  811.9 460.7 %reduce-scatter.15.cloned.1.call-start = ((), (), s32[]{:S(2)}) async-start(), calls=%async_computation.17 | async-start | bytes 2433024 | tf_op jit(solution)/shard_map/reduce_scatter | solution.py:334
  815.7 561.5 %reduce-scatter.17.cloned.1.call-start = ((), (), s32[]{:S(2)}) async-start(), calls=%async_computation.18 | async-start | bytes 2433024 | tf_op jit(solution)/shard_map/reduce_scatter | solution.py:335
  818.2 700.0 %reduce-scatter.21.cloned.1.call-start = ((), (), s32[]{:S(2)}) async-start(), calls=%async_computation.20 | async-start | bytes 9732096 | tf_op jit(solution)/shard_map/reduce_scatter | solution.py:337
  825.6 834.6 %reduce-scatter.23.cloned.1.call-start = ((), (), s32[]{:S(2)}) async-start(), calls=%async_computation.21 | async-start | bytes 9732096 | tf_op jit(solution)/shard_map/reduce_scatter | solution.py:338
  (38 other events, 92.6 us)
Sparse Core Ops, SparseCore 0:
  10.8 56.9 all-gather.10
  70.6 52.9 all-gather.14
  126.4 53.0 all-gather.12
  181.4 62.4 all-gather.22
  245.9 62.1 all-gather.24
  310.8 52.7 all-gather.16
  366.4 62.4 all-gather.18
  431.7 62.3 all-gather.20
  674.9 59.0 reduce-scatter.8
  736.2 60.2 reduce-scatter.10
  805.7 148.2 all-reduce.29
  962.0 101.9 reduce-scatter.12
  1070.7 98.0 reduce-scatter.18
  1174.5 98.0 reduce-scatter.14
  1279.1 98.0 reduce-scatter.16
  1383.5 134.6 reduce-scatter.20
  1525.5 134.5 reduce-scatter.22
where the time goes:
time: 1670 us
  waiting for transfers between devices  1240 us (74%)
  matrix products  211 us (13%)
  local copies, waits for them, and re-layouts  89.4 us (5%)
  other arithmetic  68.2 us (4%)
  blocking collectives  42.9 us (3%)
    reduce_scatter x1, waiting for transfers between devices, per_device(): lax.psum_scatter(grad_w_outer, ('dp', 'seq'), scatter_dimension=0, tiled=...  142 us
    reduce_scatter x1, waiting for transfers between devices, per_device(): lax.psum_scatter(grad_w_inner, ('dp', 'seq'), scatter_dimension=0, tiled=...  141 us
    unnamed x18, waiting for transfers between devices  116 us
    reduce_scatter x1, waiting for transfers between devices, per_device(): lax.psum_scatter(grad_w_output, ('dp', 'seq'), scatter_dimension=0, tiled...  105 us
    reduce_scatter x1, waiting for transfers between devices, per_device(): lax.psum_scatter(grad_w_value, ('dp', 'seq'), scatter_dimension=0, tiled=...  105 us
    reduce_scatter x1, waiting for transfers between devices, per_device(): lax.psum_scatter(grad_w_key, ('dp', 'seq'), scatter_dimension=0, tiled=True)  104 us
    reduce_scatter x1, waiting for transfers between devices, per_device(): lax.psum_scatter(grad_w_query, ('dp', 'seq'), scatter_dimension=0, tiled=...  93.6 us
    all_gather x1, waiting for transfers between devices, per_device(): lax.all_gather(values_own, 'seq', axis=1, tiled=True)  62 us
  transfers between devices with their start and end apart: 17, of which 16 were waited for; matrix products, arithmetic and copies ran while one was open for 11% of the time, Pallas kernels for 0%

commit v1 on v0

v1 whole, which is shorter than its diff:
```python
import functools

import jax
import jax.numpy as jnp
from jax import lax
from jax.experimental import pallas as pl
from jax.experimental.pallas import tpu as pltpu
from jax.sharding import PartitionSpec as P

HEAD = 64
BLOCK = 256
EPSILON = 1e-05
LOW = jnp.bfloat16
F32 = jnp.float32


def layer_norm(values, scaling, offset):
    centered = values - jnp.mean(values, axis=-1, keepdims=True)
    variance = jnp.mean(centered * centered, axis=-1, keepdims=True)
    return centered * lax.rsqrt(variance + EPSILON) * scaling + offset


def hidden_norm(hidden_pre, scaling, offset):
    return layer_norm(jax.nn.gelu(hidden_pre, approximate=False), scaling, offset)


def product(former, latter):
    return jnp.dot(former, latter, preferred_element_type=F32)


def product_left(former, latter):
    return jnp.einsum("ta,tb->ab", former, latter, preferred_element_type=F32)


def product_right(former, latter):
    return jnp.einsum("ta,ba->tb", former, latter, preferred_element_type=F32)


def column_sums(matrix):
    return jnp.sum(matrix.astype(F32), axis=0)


def dot_nt(former, latter):
    return lax.dot_general(former, latter, (((1,), (1,)), ((), ())), preferred_element_type=F32)


def dot_nn(former, latter):
    return lax.dot_general(former, latter, (((1,), (0,)), ((), ())), preferred_element_type=F32)


def attend_kernel(heads, blocks, qkv_ref, o_ref, ot_ref, lse_ref, qs, ks, vt):
    width = heads * HEAD
    for h in range(heads):
        qs[h] = qkv_ref[:, h * HEAD:(h + 1) * HEAD]
        ks[h] = qkv_ref[:, width + h * HEAD:width + (h + 1) * HEAD]
    vt[...] = qkv_ref[:, 2 * width:3 * width].T

    def row_block(i, unused):
        rows = pl.ds(pl.multiple_of(i * BLOCK, BLOCK), BLOCK)

        def pair(j, carried):
            cols = pl.ds(pl.multiple_of(j * BLOCK, BLOCK), BLOCK)
            result = []
            for h in range(heads):
                largest, totals, mixed = carried[3 * h:3 * h + 3]
                scores = dot_nt(ks[h, cols, :], qs[h, rows, :])
                newest = jnp.maximum(largest, jnp.max(scores, axis=0, keepdims=True))
                shrink = jnp.exp(largest - newest)
                powered = jnp.exp(scores - newest)
                totals = totals * shrink + jnp.sum(powered, axis=0, keepdims=True)
                mixed = mixed * shrink + dot_nn(vt[h * HEAD:(h + 1) * HEAD, cols], powered.astype(LOW))
                result += [newest, totals, mixed]
            return tuple(result)

        initial = []
        for h in range(heads):
            initial += [
                jnp.full((1, BLOCK), -jnp.inf, F32),
                jnp.zeros((1, BLOCK), F32),
                jnp.zeros((HEAD, BLOCK), F32),
            ]
        final = lax.fori_loop(0, i + 1, pair, tuple(initial))
        parts = []
        for h in range(heads):
            largest, totals, mixed = final[3 * h:3 * h + 3]
            attended = mixed / totals
            ot_ref[h * HEAD:(h + 1) * HEAD, rows] = attended
            lse_ref[h:h + 1, rows] = largest + jnp.log(totals)
            parts.append(attended)
        o_ref[rows, :] = jnp.concatenate(parts, axis=0).T.astype(LOW)
        return unused

    lax.fori_loop(0, blocks, row_block, 0)


def attend_back_kernel(heads, blocks, qkv_ref, do_ref, ot_ref, lse_ref, out_ref, qs, ks, vs, ds, kt, dk, dv):
    width = heads * HEAD
    for h in range(heads):
        qs[h] = qkv_ref[:, h * HEAD:(h + 1) * HEAD]
        ks[h] = qkv_ref[:, width + h * HEAD:width + (h + 1) * HEAD]
        vs[h] = qkv_ref[:, 2 * width + h * HEAD:2 * width + (h + 1) * HEAD]
        ds[h] = do_ref[:, h * HEAD:(h + 1) * HEAD]
    kt[...] = qkv_ref[:, width:2 * width].T
    dk[...] = jnp.zeros_like(dk)
    dv[...] = jnp.zeros_like(dv)

    def row_block(i, unused):
        rows = pl.ds(pl.multiple_of(i * BLOCK, BLOCK), BLOCK)
        inner = []
        for h in range(heads):
            grad_t = ds[h, rows, :].astype(F32).T
            inner.append(jnp.sum(grad_t * ot_ref[h * HEAD:(h + 1) * HEAD, rows], axis=0, keepdims=True))

        def pair(j, carried):
            cols = pl.ds(pl.multiple_of(j * BLOCK, BLOCK), BLOCK)
            result = []
            for h in range(heads):
                query, grad = qs[h, rows, :], ds[h, rows, :]
                shares = jnp.exp(dot_nt(ks[h, cols, :], query) - lse_ref[h:h + 1, rows])
                grad_shares = dot_nt(vs[h, cols, :], grad)
                grad_scores = (shares * (grad_shares - inner[h])).astype(LOW)
                dv[h, cols, :] += dot_nn(shares.astype(LOW), grad)
                dk[h, cols, :] += dot_nn(grad_scores, query)
                result.append(carried[h] + dot_nn(kt[h * HEAD:(h + 1) * HEAD, cols], grad_scores))
            return tuple(result)

        final = lax.fori_loop(0, i + 1, pair, tuple(jnp.zeros((HEAD, BLOCK), F32) for unused in range(heads)))
        grad_query = jnp.concatenate(final, axis=0).T * HEAD ** (-0.5)
        out_ref[rows, 0:width] = grad_query.astype(LOW)
        return unused

    lax.fori_loop(0, blocks, row_block, 0)
    for h in range(heads):
        out_ref[:, width + h * HEAD:width + (h + 1) * HEAD] = dk[h].astype(LOW)
        out_ref[:, 2 * width + h * HEAD:2 * width + (h + 1) * HEAD] = dv[h].astype(LOW)


def whole_vmem(count):
    return [pl.BlockSpec(memory_space=pltpu.VMEM)] * count


def attend_forward(qkv, heads):
    length = qkv.shape[0]
    width = heads * HEAD
    return pl.pallas_call(
        functools.partial(attend_kernel, heads, length // BLOCK),
        out_shape=(
            jax.ShapeDtypeStruct((length, width), LOW),
            jax.ShapeDtypeStruct((width, length), F32),
            jax.ShapeDtypeStruct((heads, length), F32),
        ),
        in_specs=whole_vmem(1),
        out_specs=tuple(whole_vmem(3)),
        scratch_shapes=[
            pltpu.VMEM((heads, length, HEAD), LOW),
            pltpu.VMEM((heads, length, HEAD), LOW),
            pltpu.VMEM((width, length), LOW),
        ],
        name="attend_forward",
    )(qkv)


def attend_backward(qkv, grad_attended, attended_t, logsum, heads):
    length = qkv.shape[0]
    width = heads * HEAD
    return pl.pallas_call(
        functools.partial(attend_back_kernel, heads, length // BLOCK),
        out_shape=jax.ShapeDtypeStruct((length, 3 * width), LOW),
        in_specs=whole_vmem(4),
        out_specs=whole_vmem(1)[0],
        scratch_shapes=[pltpu.VMEM((heads, length, HEAD), LOW)] * 4
        + [pltpu.VMEM((width, length), LOW)]
        + [pltpu.VMEM((heads, length, HEAD), F32)] * 2,
        name="attend_backward",
    )(qkv, grad_attended, attended_t, logsum)


def exchange(values, axis, bit):
    size = lax.axis_size(axis)
    return lax.ppermute(values, axis, [(i, i ^ (1 << bit)) for i in range(size)])


def bit_of(axis, bit):
    return (lax.axis_index(axis) >> bit) & 1


def bit_order(axis):
    count = lax.axis_size(axis).bit_length() - 1
    return count, list(range(1, count)) + [0]


def gather_tree(values, axis):
    count, order = bit_order(axis)
    for bit in order:
        other = exchange(values, axis, bit)
        first = bit_of(axis, bit) == 0
        values = jnp.stack([jnp.where(first, values, other), jnp.where(first, other, values)])
    where_is = {bit: len(order) - 1 - place for place, bit in enumerate(order)}
    axes = [where_is[bit] for bit in reversed(range(count))]
    rest = list(range(count, values.ndim))
    values = jnp.transpose(values, axes + rest)
    return values.reshape((1 << count,) + values.shape[count:])


def scatter_tree(values, axis):
    count, order = bit_order(axis)
    payload = values.shape[1:]
    values = values.reshape((2,) * count + payload)
    left = list(reversed(range(count)))
    for bit in reversed(order):
        place = left.index(bit)
        left.remove(bit)
        mine = bit_of(axis, bit)
        kept = lax.dynamic_index_in_dim(values, mine, place, keepdims=False)
        sent = lax.dynamic_index_in_dim(values, 1 - mine, place, keepdims=False)
        got = exchange(sent.astype(LOW), axis, bit)
        values = kept.astype(F32) + got.astype(F32)
    return values


def gather_neighbours(values, axis):
    size = lax.axis_size(axis)
    place = lax.axis_index(axis)
    upward = [values]
    downward = [values]
    for step in range(1, size):
        upward.append(lax.ppermute(upward[-1], axis, [(i, i + 1) for i in range(size - 1)]))
        downward.append(lax.ppermute(downward[-1], axis, [(i + 1, i) for i in range(size - 1)]))
    pieces = [values]
    for step in range(1, size):
        pieces.append(jnp.where(place >= step, upward[step], downward[size - step]))
    return pieces


def spread(values, axis):
    return lax.all_to_all(values, axis, 0, 0, tiled=True)


def per_device(
    tokens,
    cotangent,
    w_query,
    w_key,
    w_value,
    w_output,
    w_inner,
    w_outer,
    bias_query,
    bias_value,
    bias_output,
    bias_inner,
    bias_outer,
    gain_input,
    bias_input,
    gain_attend,
    bias_attend,
    gain_middle,
    bias_middle,
    gain_hidden,
    bias_hidden,
):
    seq_size, dp_size = lax.axis_size("seq"), lax.axis_size("dp")
    devices = seq_size * dp_size
    place = lax.axis_index("seq")
    groups, rows, width = tokens.shape
    count = groups * rows
    length = seq_size * rows
    all_heads = width // HEAD
    heads = groups * all_heads // seq_size
    parts = all_heads // heads
    part_width = heads * HEAD
    own_rows = w_query.shape[0]
    ff = w_inner.shape[1]
    ratio = ff // width

    packed_weights = jnp.concatenate(
        [w_output]
        + [w_inner[:, c * width:(c + 1) * width] for c in range(ratio)]
        + [w_outer, w_query, w_key, w_value],
        axis=0,
    )
    weights = lax.all_gather(packed_weights, ("dp", "seq"), axis=0, tiled=False)

    vectors = (
        bias_query, bias_value, bias_output, bias_inner, bias_outer, gain_input, bias_input,
        gain_attend, bias_attend, gain_middle, bias_middle, gain_hidden, bias_hidden,
    )
    columns = jnp.stack([w_query, w_key, w_value]).reshape(3, own_rows, parts, part_width)
    columns = jnp.transpose(columns, (2, 1, 0, 3)).reshape(parts, own_rows, 3 * part_width)
    flat = jnp.concatenate(vectors)
    extra = -(-flat.shape[0] // (3 * part_width))
    flat = jnp.pad(flat, (0, extra * 3 * part_width - flat.shape[0])).reshape(1, extra, 3 * part_width)
    first = jnp.concatenate([columns, jnp.broadcast_to(flat, (parts, extra, 3 * part_width))], axis=1)
    first = jnp.tile(first, (groups, 1, 1))
    first = gather_tree(spread(first, "seq"), "dp").reshape(devices, own_rows + extra, 3 * part_width)
    w_own = first[:, :own_rows].reshape(width, 3 * part_width)
    flat = first[:, own_rows:].reshape(devices, extra * 3 * part_width).astype(F32)
    full = []
    offset = 0
    for member in vectors:
        size = member.shape[0]
        full.append(flat[:, offset:offset + size].reshape(devices * size))
        offset += size
    (
        bq_full, bv_full, bo_full, bi_full, bu_full, gin_full, bin_full,
        gat_full, bat_full, gmi_full, bmi_full, ghi_full, bhi_full,
    ) = full

    own_group, own_part = place // parts, place % parts
    pieces = gather_neighbours(tokens, "seq")
    normed_all = jnp.zeros((seq_size, rows, width), LOW)
    for step, piece in enumerate(pieces):
        chosen = lax.dynamic_index_in_dim(piece, own_group, 0, keepdims=False) if groups > 1 else piece[0]
        normed = layer_norm(chosen.astype(F32), gin_full, bin_full).astype(LOW)
        normed_all = lax.dynamic_update_index_in_dim(normed_all, normed, (place - step) % seq_size, 0)
    normed_all = normed_all.reshape(length, width)
    bq_own = lax.dynamic_slice_in_dim(bq_full, own_part * part_width, part_width, 0)
    bv_own = lax.dynamic_slice_in_dim(bv_full, own_part * part_width, part_width, 0)
    bias_own = jnp.concatenate([bq_own, jnp.zeros_like(bq_own), bv_own])
    scale_own = jnp.concatenate(
        [jnp.full((part_width,), HEAD ** (-0.5), LOW), jnp.ones((2 * part_width,), LOW)]
    )
    qkv = (product(normed_all, w_own) + bias_own).astype(LOW) * scale_own
    attended_low, attended_t, logsum = attend_forward(qkv, heads)

    def to_rows(values, per):
        received = spread(values.reshape(seq_size, rows, per), "seq").reshape(groups, parts, rows, per)
        return received

    attended = jnp.transpose(to_rows(attended_low, part_width), (0, 2, 1, 3)).reshape(count, width).astype(F32)

    w_output_full = weights[:, :own_rows].reshape(width, width)
    at = own_rows
    w_inner_full = [weights[:, at + c * own_rows:at + (c + 1) * own_rows].reshape(width, width) for c in range(ratio)]
    w_inner_full = jnp.concatenate(w_inner_full, axis=1)
    at += ratio * own_rows
    w_outer_full = weights[:, at:at + ratio * own_rows].reshape(ff, width)
    at += ratio * own_rows
    w_qkv_full = [weights[:, at + c * own_rows:at + (c + 1) * own_rows].reshape(width, width) for c in range(3)]

    inputs = tokens.astype(F32).reshape(count, width)
    sub_low, pull_attend = jax.vjp(layer_norm, attended, gat_full, bat_full)
    sub_low = sub_low.astype(LOW)
    middle = inputs + product(sub_low, w_output_full) + bo_full
    normed_mid, pull_middle = jax.vjp(layer_norm, middle, gmi_full, bmi_full)
    normed_mid = normed_mid.astype(LOW)
    hidden_pre = product(normed_mid, w_inner_full) + bi_full
    hidden_low, pull_hidden = jax.vjp(hidden_norm, hidden_pre, ghi_full, bhi_full)
    hidden_low = hidden_low.astype(LOW)
    output = (middle + product(hidden_low, w_outer_full) + bu_full).astype(LOW)

    cotangent_flat = cotangent.reshape(count, width)
    grad_w_outer = product_left(hidden_low, cotangent_flat)
    grad_bias_outer = column_sums(cotangent_flat)
    grad_pre, grad_gain_hidden, grad_bias_hidden = pull_hidden(product_right(cotangent_flat, w_outer_full))
    grad_pre_low = grad_pre.astype(LOW)
    grad_w_inner = product_left(normed_mid, grad_pre_low)
    grad_bias_inner = column_sums(grad_pre_low)
    grad_mid_part, grad_gain_middle, grad_bias_middle = pull_middle(product_right(grad_pre_low, w_inner_full))
    grad_middle = cotangent_flat.astype(F32) + grad_mid_part
    grad_branch = grad_middle.astype(LOW)
    grad_w_output = product_left(sub_low, grad_branch)
    grad_bias_output = column_sums(grad_branch)
    grad_att, grad_gain_attend, grad_bias_attend = pull_attend(product_right(grad_branch, w_output_full))

    def packed_vectors(members, row_width):
        joined = jnp.concatenate([member.reshape(devices, -1) for member in members], axis=1)
        row_count = -(-joined.shape[1] // row_width)
        joined = jnp.pad(joined, ((0, 0), (0, row_count * row_width - joined.shape[1])))
        return joined.reshape(devices, row_count, row_width).astype(LOW)

    def unpacked(flat, sizes):
        result, offset = [], 0
        for size in sizes:
            result.append(flat[offset:offset + size])
            offset += size
        return result

    early = (
        grad_bias_output, grad_bias_inner, grad_bias_outer, grad_gain_attend, grad_bias_attend,
        grad_gain_middle, grad_bias_middle, grad_gain_hidden, grad_bias_hidden,
    )
    packed = jnp.concatenate(
        [
            grad_w_outer.astype(LOW).reshape(devices, ratio * own_rows, width),
            grad_w_inner.astype(LOW).reshape(devices, ratio * own_rows, width),
            grad_w_output.astype(LOW).reshape(devices, own_rows, width),
            packed_vectors(early, width),
        ],
        axis=1,
    )
    summed = lax.psum_scatter(packed, ("dp", "seq"), scatter_dimension=0, tiled=True)[0].astype(F32)

    grad_att_low = jnp.transpose(grad_att.astype(LOW).reshape(groups, rows, parts, part_width), (0, 2, 1, 3))
    grad_att_own = spread(grad_att_low.reshape(seq_size, rows, part_width), "seq").reshape(length, part_width)
    grad_qkv = attend_backward(qkv, grad_att_own, attended_t, logsum, heads)
    grad_w_own = product_left(normed_all, grad_qkv)

    received = to_rows(grad_qkv, 3 * part_width).reshape(groups, parts, rows, 3, part_width)
    received = jnp.transpose(received, (3, 0, 2, 1, 4)).reshape(3, count, width)
    grad_normed = (
        product_right(received[0], w_qkv_full[0])
        + product_right(received[1], w_qkv_full[1])
        + product_right(received[2], w_qkv_full[2])
    )
    grad_bias_query = column_sums(received[0])
    grad_bias_value = column_sums(received[2])
    unused, pull_input = jax.vjp(layer_norm, inputs, gin_full, bin_full)
    grad_in_part, grad_gain_input, grad_bias_input = pull_input(grad_normed)
    grad_tokens = (grad_middle + grad_in_part).reshape(groups, rows, width)

    late = (grad_bias_query, grad_bias_value, grad_gain_input, grad_bias_input)
    late_packed = packed_vectors(late, 3 * part_width)
    last = jnp.concatenate(
        [grad_w_own.astype(LOW).reshape(devices, own_rows, 3 * part_width), late_packed], axis=1
    )
    last_rows = last.shape[1]
    last = scatter_tree(last.reshape(dp_size, seq_size, last_rows, 3 * part_width), "dp")
    last = spread(last.astype(LOW), "seq").astype(F32)
    grad_own = jnp.sum(last[:, :own_rows].reshape(groups, parts, own_rows, 3, part_width), axis=0)
    grad_own = jnp.transpose(grad_own, (2, 1, 0, 3)).reshape(3, own_rows, width)
    late_flat = jnp.sum(last[:, own_rows:], axis=0).reshape(-1)
    own_ff = ratio * own_rows
    gbq, gbv, ggi, gbi = unpacked(late_flat, [own_rows] * 4)
    gbo, gbin, gbu, gga, gba, ggm, gbm, ggh, gbh = unpacked(
        summed[2 * own_ff + own_rows:].reshape(-1),
        [own_rows, own_ff, own_rows, own_rows, own_rows, own_rows, own_rows, own_ff, own_ff],
    )
    return (
        output.reshape(groups, rows, width),
        grad_tokens,
        grad_own[0],
        grad_own[1],
        grad_own[2],
        summed[2 * own_ff:2 * own_ff + own_rows],
        summed[own_ff:2 * own_ff].reshape(own_rows, ff),
        summed[:own_ff],
        gbq,
        gbv,
        gbo,
        gbin,
        gbu,
        ggi,
        gbi,
        gga,
        gba,
        ggm,
        gbm,
        ggh,
        gbh,
    )


def solution(mesh):
    rows3 = P("dp", "seq", None)
    split2 = P(("dp", "seq"), None)
    split1 = P(("dp", "seq"))
    return jax.shard_map(
        per_device,
        mesh=mesh,
        in_specs=(rows3,) * 2 + (split2,) * 6 + (split1,) * 13,
        out_specs=(rows3,) * 2 + (split2,) * 6 + (split1,) * 13,
        check_vma=False,
    )
```

time: 1670 us -> 538 us (0.32)
  waiting for transfers between devices: 1240 us -> 181 us
  matrix products: 211 us -> 67.5 us
  Pallas kernels: 0 us -> 82.7 us
  starting transfers between devices: 1.36 us -> 37.7 us
  local copies, waits for them, and re-layouts: 89.4 us -> 62.1 us
  other arithmetic: 68.2 us -> 51.5 us
    reduce_scatter x8 -> x1, waiting for transfers between devices: 803 us -> 0.01 us  [per_device(): lax.psum_scatter(packed, ('dp', 'seq'), scatter_dimension=0, tiled=True)[0]]
    all_gather x8 -> x1, waiting for transfers between devices: 319 us -> 0.02 us  [per_device(): weights = lax.all_gather(packed_weights, ('dp', 'seq'), axis=0, tiled=False)]
    dot_general x60 -> x14, matrix products: 211 us -> 67.5 us  [the longest x4 32.3 us: product(): return jnp.dot(former, latter, preferred_element_type=F32)]
    unnamed x18 -> x2, waiting for transfers between devices: 116 us -> 0.03 us
    ppermute x0 -> x12, waiting for transfers between devices: none -> 95.1 us  [the longest x3 82.9 us: gather_neighbours(): lax.ppermute(downward[-1], axis, [(i + 1, i) for i in range(size - 1)])]
    all_to_all x0 -> x3, waiting for transfers between devices: none -> 86.3 us  [spread(): return lax.all_to_all(values, axis, 0, 0, tiled=True)]
    pallas_call x0 -> x2, Pallas kernels: none -> 82.7 us  [the longest x1 41.5 us: attend_backward(): pl.pallas_call(functools.partial(attend_back_kernel, heads, length // BLO...]
    unnamed x1 -> x0, blocking collectives: 42.9 us -> none
  transfers between devices with their start and end apart: 17 -> 17, of which waited for: 16 -> 11; matrix products, arithmetic and copies ran while one was open for 11% -> 13% of each run, Pallas kernels for 0% -> 16%
where the time goes in v1:
time: 538 us; the launch traced here: 531 us
  waiting for transfers between devices  181 us (34%)
  Pallas kernels  82.7 us (15%)
  matrix products  67.5 us (13%)
  local copies, waits for them, and re-layouts  62.1 us (12%)
  other arithmetic  51.5 us (10%)
  starting transfers between devices  37.7 us (7%)
  blocking collectives  31.9 us (6%)
  between operations  15.8 us (3%)
    all_to_all x3, waiting for transfers between devices, spread(): return lax.all_to_all(values, axis, 0, 0, tiled=True)  86.3 us
    ppermute x3, waiting for transfers between devices, gather_neighbours(): lax.ppermute(downward[-1], axis, [(i + 1, i) for i in range(size - 1)])  82.9 us
    pallas_call x1, Pallas kernels, attend_backward(): pl.pallas_call(functools.partial(attend_back_kernel, heads, length // BLO...  41.5 us
    pallas_call x1, Pallas kernels, attend_forward(): pl.pallas_call(functools.partial(attend_kernel, heads, length // BLOCK),...  41.2 us
    dot_general x4, matrix products, product(): return jnp.dot(former, latter, preferred_element_type=F32)  32.3 us
    all_to_all x2, blocking collectives, spread(): return lax.all_to_all(values, axis, 0, 0, tiled=True)  31.9 us
    dot_general x6, matrix products, product_right(): return jnp.einsum('ta,ba->tb', former, latter, preferred_element_type=F32)  17.8 us
    dot_general x4, matrix products, product_left(): return jnp.einsum('ta,tb->ab', former, latter, preferred_element_type=F32)  17.4 us
  transfers between devices with their start and end apart: 17, of which 11 were waited for; matrix products, arithmetic and copies ran while one was open for 13% of the time, Pallas kernels for 16%

profile of v1, /device:TPU:0, one launch (start us, length us, event | category | flops | bytes accessed | tf_op | source)
XLA Modules:
  0.0 530.8 jit_solution(17825701305054408432)
XLA Ops:
  19.0 15.3 %all_to_all.25 = bf16[4,25,576]{2,1,0:T(8,128)(2,1)S(1)} all-to-all(bf16[4,25,576]{2,1,0:T(8,128)(2,1)S(1)} %pad_maximum_fusion.6), channel_id=1, replica_groups=mesh['dp'=8,'seq'=4] {'seq'}, dimensions={0} | all-to-all | bytes 230400 | tf_op jit(solution)/shard_map/all_to_all | solution.py:236
  34.3 1.5 collective-permute-start
  35.8 3.8 collective-permute-done
  39.8 1.7 collective-permute-start.1
  41.4 1.3 collective-permute-start.4
  42.7 5.5 %collective-permute-start.3 = (bf16[1,512,768]{2,1,0:T(8,128)(2,1)S(1)}, bf16[1,512,768]{2,1,0:T(8,128)(2,1)}, u32[]{:S(2)}, u32[]{:S(2)}) collective-permute-start(bf16[1,512,768]{2,1,0:T(8,128)(2,1)S(1)} %copy-done), channel_id=1, source_target_pairs={{0,1},{1,2},{2,3},{4,5},{5,6},{6,7},{8,9},{9,10},{10,11},{12,13},{... | collective-permute-start | bytes 2359304 | tf_op jit(solution)/shard_map/ppermute | solution.py:227
  49.4 32.0 %collective-permute-done.4 = bf16[1,512,768]{2,1,0:T(8,128)(2,1)} collective-permute-done((bf16[1,512,768]{2,1,0:T(8,128)(2,1)S(1)}, bf16[1,512,768]{2,1,0:T(8,128)(2,1)}, u32[]{:S(2)}, u32[]{:S(2)}) %collective-permute-start.4) | collective-permute-done | bytes 786464 | tf_op jit(solution)/shard_map/ppermute | solution.py:228
  81.4 1.3 collective-permute-start.5
  82.7 5.5 %collective-permute-start.7 = (bf16[1,512,768]{2,1,0:T(8,128)(2,1)}, bf16[1,512,768]{2,1,0:T(8,128)(2,1)}, u32[]{:S(2)}, u32[]{:S(2)}) collective-permute-start(bf16[1,512,768]{2,1,0:T(8,128)(2,1)} %collective-permute-done.3), channel_id=1, source_target_pairs={{0,1},{1,2},{2,3},{4,5},{5,6},{6,7},{8,9},{9,10},{10,11},{12,13},{... | collective-permute-start | bytes 2359304 | tf_op jit(solution)/shard_map/ppermute | solution.py:227
  91.5 31.3 %collective-permute-done.5 = bf16[1,512,768]{2,1,0:T(8,128)(2,1)} collective-permute-done((bf16[1,512,768]{2,1,0:T(8,128)(2,1)}, bf16[1,512,768]{2,1,0:T(8,128)(2,1)}, u32[]{:S(2)}, u32[]{:S(2)}) %collective-permute-start.5) | collective-permute-done | bytes 786464 | tf_op jit(solution)/shard_map/ppermute | solution.py:228
  122.8 1.3 collective-permute-start.6
  124.1 4.8 collective-permute-start.8
  128.9 1.5 convert_reduce_fusion.1
  130.7 19.6 %collective-permute-done.6 = bf16[1,512,768]{2,1,0:T(8,128)(2,1)S(1)} collective-permute-done((bf16[1,512,768]{2,1,0:T(8,128)(2,1)}, bf16[1,512,768]{2,1,0:T(8,128)(2,1)S(1)}, u32[]{:S(2)}, u32[]{:S(2)}) %collective-permute-start.6) | collective-permute-done | bytes 786464 | tf_op jit(solution)/shard_map/ppermute | solution.py:228
  151.8 1.4 convert_reduce_fusion
  154.7 1.6 copy-done.12
  156.4 3.9 fusion.8.qkv_ref
  160.2 41.2 %attend_forward.1 = (bf16[2048,192]{1,0:T(8,128)(2,1)}, f32[192,2048]{1,0:T(8,128)}, f32[3,2048]{1,0:T(4,128)}) custom-call(bf16[2048,576]{1,0:T(8,128)(2,1)} %fusion.8.qkv_ref), custom_call_target="tpu_custom_call" | custom-call | tf_op jit(solution)/shard_map/attend_forward/pallas_call | solution.py:145
  201.4 2.3 copy.126
  203.7 3.8 all-to-all-start.1
  208.6 11.9 %all-to-all-done.1 = bf16[4,512,192]{1,2,0:T(8,128)(2,1)S(1)} async-done(((bf16[4,512,192]{1,2,0:T(8,128)(2,1)}), bf16[4,512,192]{1,2,0:T(8,128)(2,1)S(1)}, u32[]{:S(2)}, u32[]{:S(2)}) %all-to-all-start.1) | async-done | bytes 786464 | tf_op jit(solution)/shard_map/all_to_all | solution.py:236
  220.5 1.4 convert_element_type.194
  221.9 3.0 copy.127
  225.7 2.6 slice.306
  228.4 7.3 %fusion.88 = (bf16[32,24,768]{2,1,0:T(8,128)(2,1)}, bf16[32,24,768]{2,1,0:T(8,128)(2,1)}, bf16[32,24,768]{2,1,0:T(8,128)(2,1)}, bf16[32,24,768]{2,1,0:T(8,128)(2...) fusion(bf16[32,288,768]{2,1,0:T(8,128)(2,1)} %bitcast.228), kind=kLoop, calls=%fused_computation.219 | loop fusion | bytes 18874368 | tf_op jit(solution)/shard_map/slice | solution.py:339
  238.2 20.7 %fusion.86 = (f32[512]{0:T(512)S(1)}, f32[512,3072]{1,0:T(8,128)S(1)}, f32[512,3072]{1,0:T(8,128)}, f32[512,3072]{1,0:T(8,128)}) fusion(f32[3072]{0:T(1024)S(1)} %add.303, bf16[768,768]{1,0:T(8,128)(2,1)S(1)} %bitcast.247, bf16[768,768]{1,0:T(8,128)(2,1)S(1)} %bitcast.249, bf16[768,768]{1,0:T(8,128)(2,1)S(1)} %bitcast.251, ...), kind=kOutput, calls=%fused_computation.218 | convolution fusion | flops 2540568064 | bytes 25190400 | tf_op jit(solution)/shard_map/dot_general | solution.py:28
  259.0 5.0 multiply_reduce_fusion
  264.0 3.2 reduce_sum.384
  267.3 7.5 %fusion.1 = (bf16[3072]{0:T(1024)(128)(2,1)S(1)}, f32[512]{0:T(512)S(1)}, bf16[512,3072]{1,0:T(8,128)(2,1)}) fusion(f32[3072,512]{0,1:T(8,128)} %get-tuple-element.113, f32[512,3072]{1,0:T(8,128)} %copy-done.1, f32[512]{0:T(512)S(1)} %get-tuple-element.109, f32[512]{0:T(512)S(1)} %broadcast_multiply_fusion, f32[512]{0:T(512)S(1)} %get-tuple-element.108, ...), kind=kLoop, calls=%fused_computation.6 | loop fusion | flops 20443648 | bytes 15767552 | tf_op jit(solution)/shard_map/transpose(jvp())/reduce_sum | solution.py:20
  274.8 1.3 slice-done.3
  276.1 8.5 %fusion.81 = (bf16[3072]{0:T(1024)(128)(2,1)S(1)}, bf16[512,3072]{1,0:T(8,128)(2,1)S(1)}) fusion(f32[512,3072]{1,0:T(8,128)} %get-tuple-element.52, f32[512]{0:T(512)S(1)} %negate_multiply_fusion.4, f32[512]{0:T(512)S(1)} %get-tuple-element.108, f32[512,3072]{1,0:T(8,128)S(1)} %bitcast.224, f32[512]{0:T(512)S(1)} %broadcast_multiply_fusion, ...), kind=kLoop, calls=%fused_computation.214 | loop fusion | flops 36172800 | bytes 28350464 | tf_op jit(solution)/shard_map/reduce_sum | solution.py:40
  284.7 4.0 multiply_reduce_fusion.2
  288.7 4.9 convolution_convert_fusion
  293.8 2.5 fusion.85
  296.3 8.7 %reshape.609 = bf16[32,96,768]{2,1,0:T(8,128)(2,1)} reshape(bf16[768,3072]{1,0:T(8,128)(2,1)} %convolution_convert_fusion) | data formatting | bytes 9437184 | tf_op jit(solution)/shard_map/reshape | solution.py:386
  305.3 1.2 fusion.82
  306.6 4.3 multiply_reduce_fusion.3
  310.9 2.1 convolution_convert_fusion.2
  313.5 4.7 convolution_convert_fusion.1
  318.2 5.3 pad_maximum_fusion
  323.5 2.5 fusion.84
  326.2 1.2 copy.128
  327.3 16.6 %all_to_all.26 = bf16[4,512,192]{1,2,0:T(8,128)(2,1)S(1)} all-to-all(bf16[4,512,192]{1,2,0:T(8,128)(2,1)} %bitcast.238), channel_id=1, replica_groups=mesh['dp'=8,'seq'=4] {'seq'}, dimensions={0} | all-to-all | bytes 1572864 | tf_op jit(solution)/shard_map/all_to_all | solution.py:236
  343.9 1.3 copy.129
  345.2 41.5 %attend_backward.1 = bf16[2048,576]{1,0:T(8,128)(2,1)} custom-call(bf16[2048,576]{1,0:T(8,128)(2,1)} %fusion.8.qkv_ref, bf16[2048,192]{1,0:T(8,128)(2,1)} %bitcast.237, f32[192,2048]{1,0:T(8,128)} %get-tuple-element.25.ot_ref, f32[3,2048]{1,0:T(4,128)} %get-tuple-element.26.lse_ref), custom_call_target="tpu_custom_call" | custom-call | tf_op jit(solution)/shard_map/attend_backward/pallas_call | solution.py:166
  386.7 4.4 copy.130
  391.1 4.7 all-to-all-start.3
  395.8 5.7 %convolution_convert_fusion.3 = bf16[768,576]{0,1:T(8,128)(2,1)} fusion(bf16[2048,768]{1,0:T(8,128)(2,1)} %bitcast.240, bf16[2048,576]{1,0:T(8,128)(2,1)} %attend_backward.1), kind=kOutput, calls=%fused_computation.100 | convolution fusion | flops 1812381696 | bytes 6389760 | tf_op jit(solution)/shard_map/ta,tb->ab/dot_general | solution.py:32
  401.5 1.5 copy.131
  403.0 71.6 %all-to-all-done.3 = bf16[4,512,576]{1,2,0:T(8,128)(2,1)} async-done(((bf16[4,512,576]{1,2,0:T(8,128)(2,1)}), bf16[4,512,576]{1,2,0:T(8,128)(2,1)}, u32[]{:S(2)}, u32[]{:S(2)}) %all-to-all-start.3) | async-done | bytes 2359328 | tf_op jit(solution)/shard_map/all_to_all | solution.py:236
  474.6 3.1 slice_reduce_fusion.2
  477.9 2.5 fusion.94
  481.9 1.2 fusion.16
  486.7 2.1 collective-permute-done.9
  488.8 1.2 convert_add_fusion
  490.1 1.5 collective-permute-start.10
  491.6 6.8 %fusion.45 = bf16[1,512,768]{2,1,0:T(8,128)(2,1)} fusion(f32[512,768]{1,0:T(8,128)S(1)} %copy-done.8, bf16[512,3072]{1,0:T(8,128)(2,1)} %get-tuple-element.67, bf16[3072,768]{1,0:T(8,128)(2,1)} %bitcast.235, f32[768]{0:T(1024)S(1)} %add.311), kind=kOutput, calls=%fused_computation.105 | convolution fusion | flops 2417098752 | bytes 10226688 | tf_op jit(solution)/shard_map/dot_general | solution.py:28
  498.4 1.5 collective-permute-done.10
  500.0 1.5 collective-permute-start.11
  501.5 4.0 collective-permute-done.11
  506.2 3.3 all-to-all-start.4
  509.6 3.2 add_bitcast_fusion
  512.8 2.7 all-to-all-done.4
  519.0 1.1 convert_bitcast_fusion.4
  (250 shorter events, 37.6 us)
Async XLA Ops:
  7.2 11.6 %copy-start.41 = (bf16[96]{0:T(256)(128)(2,1)S(1)}, bf16[96]{0:T(256)(128)(2,1)}, u32[]{:S(2)}) copy-start(bf16[96]{0:T(256)(128)(2,1)} %param.41) | copy-start | bytes 580
  7.2 11.6 %copy-start.40 = (bf16[96]{0:T(256)(128)(2,1)S(1)}, bf16[96]{0:T(256)(128)(2,1)}, u32[]{:S(2)}) copy-start(bf16[96]{0:T(256)(128)(2,1)} %param.40) | copy-start | bytes 580
  7.2 11.6 %copy-start.39 = (bf16[24]{0:T(256)(128)(2,1)S(1)}, bf16[24]{0:T(256)(128)(2,1)}, u32[]{:S(2)}) copy-start(bf16[24]{0:T(256)(128)(2,1)} %param.39) | copy-start | bytes 148
  7.2 11.6 %copy-start.38 = (bf16[24]{0:T(256)(128)(2,1)S(1)}, bf16[24]{0:T(256)(128)(2,1)}, u32[]{:S(2)}) copy-start(bf16[24]{0:T(256)(128)(2,1)} %param.38) | copy-start | bytes 148
  7.2 11.6 %copy-start.37 = (bf16[24]{0:T(256)(128)(2,1)S(1)}, bf16[24]{0:T(256)(128)(2,1)}, u32[]{:S(2)}) copy-start(bf16[24]{0:T(256)(128)(2,1)} %param.37) | copy-start | bytes 148
  7.2 11.6 %copy-start.36 = (bf16[24]{0:T(256)(128)(2,1)S(1)}, bf16[24]{0:T(256)(128)(2,1)}, u32[]{:S(2)}) copy-start(bf16[24]{0:T(256)(128)(2,1)} %param.36) | copy-start | bytes 148
  7.3 11.6 %copy-start.35 = (bf16[24]{0:T(256)(128)(2,1)S(1)}, bf16[24]{0:T(256)(128)(2,1)}, u32[]{:S(2)}) copy-start(bf16[24]{0:T(256)(128)(2,1)} %param.35) | copy-start | bytes 148
  7.3 11.6 %copy-start.34 = (bf16[24]{0:T(256)(128)(2,1)S(1)}, bf16[24]{0:T(256)(128)(2,1)}, u32[]{:S(2)}) copy-start(bf16[24]{0:T(256)(128)(2,1)} %param.34) | copy-start | bytes 148
  7.3 11.6 %copy-start.33 = (bf16[24]{0:T(256)(128)(2,1)S(1)}, bf16[24]{0:T(256)(128)(2,1)}, u32[]{:S(2)}) copy-start(bf16[24]{0:T(256)(128)(2,1)} %param.33) | copy-start | bytes 148
  7.3 11.6 %copy-start.32 = (bf16[96]{0:T(256)(128)(2,1)S(1)}, bf16[96]{0:T(256)(128)(2,1)}, u32[]{:S(2)}) copy-start(bf16[96]{0:T(256)(128)(2,1)} %param.32) | copy-start | bytes 580
  7.3 11.6 %copy-start.31 = (bf16[24]{0:T(256)(128)(2,1)S(1)}, bf16[24]{0:T(256)(128)(2,1)}, u32[]{:S(2)}) copy-start(bf16[24]{0:T(256)(128)(2,1)} %param.31) | copy-start | bytes 148
  7.3 11.6 %copy-start.30 = (bf16[24]{0:T(256)(128)(2,1)S(1)}, bf16[24]{0:T(256)(128)(2,1)}, u32[]{:S(2)}) copy-start(bf16[24]{0:T(256)(128)(2,1)} %param.30) | copy-start | bytes 148
  7.3 11.6 %copy-start.29 = (bf16[24]{0:T(256)(128)(2,1)S(1)}, bf16[24]{0:T(256)(128)(2,1)}, u32[]{:S(2)}) copy-start(bf16[24]{0:T(256)(128)(2,1)} %param.29) | copy-start | bytes 148
  7.3 218.4 %all-gather.3.cloned.1.call-start = ((), (), s32[]{:S(2)}) async-start(), calls=%async_computation.7 | async-start | bytes 14598144 | tf_op jit(solution)/shard_map/all_gather | solution.py:282
  18.0 23.4 %copy-start = (bf16[1,512,768]{2,1,0:T(8,128)(2,1)S(1)}, bf16[1,512,768]{2,1,0:T(8,128)(2,1)}, u32[]{:S(2)}) copy-start(bf16[1,512,768]{2,1,0:T(8,128)(2,1)} %param.21) | copy-start | bytes 2359300
  34.3 5.3 %collective-permute-start = (bf16[4,25,576]{2,1,0:T(8,128)(2,1)S(1)}, bf16[4,25,576]{2,1,0:T(8,128)(2,1)S(1)}, u32[]{:S(2)}, u32[]{:S(2)}) collective-permute-start(bf16[4,25,576]{2,1,0:T(8,128)(2,1)S(1)} %all_to_all.25), channel_id=1, source_target_pairs={{0,8},{4,12},{8,0},{12,4},{16,24},{20,28},{24,16},{28,20},{1,9},{5... | collective-permute-start | bytes 345608 | tf_op jit(solution)/shard_map/ppermute | solution.py:180
  39.8 8.6 %collective-permute-start.1 = (bf16[2,4,25,576]{3,2,1,0:T(8,128)(2,1)S(1)}, bf16[2,4,25,576]{3,2,1,0:T(8,128)(2,1)S(1)}, u32[]{:S(2)}, u32[]{:S(2)}) collective-permute-start(bf16[2,4,25,576]{3,2,1,0:T(8,128)(2,1)S(1)} %pad_maximum_fusion.5), channel_id=1, source_target_pairs={{0,16},{4,20},{8,24},{12,28},{16,0},{20,4},{24,8},{28,12},{1,17},{... | collective-permute-start | bytes 691208 | tf_op jit(solution)/shard_map/ppermute | solution.py:180
  41.4 40.0 %collective-permute-start.4 = (bf16[1,512,768]{2,1,0:T(8,128)(2,1)S(1)}, bf16[1,512,768]{2,1,0:T(8,128)(2,1)}, u32[]{:S(2)}, u32[]{:S(2)}) collective-permute-start(bf16[1,512,768]{2,1,0:T(8,128)(2,1)S(1)} %copy-done), channel_id=1, source_target_pairs={{1,0},{2,1},{3,2},{5,4},{6,5},{7,6},{9,8},{10,9},{11,10},{13,12},{... | collective-permute-start | bytes 2359304 | tf_op jit(solution)/shard_map/ppermute | solution.py:228
  42.7 40.0 %collective-permute-start.3 = (bf16[1,512,768]{2,1,0:T(8,128)(2,1)S(1)}, bf16[1,512,768]{2,1,0:T(8,128)(2,1)}, u32[]{:S(2)}, u32[]{:S(2)}) collective-permute-start(bf16[1,512,768]{2,1,0:T(8,128)(2,1)S(1)} %copy-done), channel_id=1, source_target_pairs={{0,1},{1,2},{2,3},{4,5},{5,6},{6,7},{8,9},{9,10},{10,11},{12,13},{... | collective-permute-start | bytes 2359304 | tf_op jit(solution)/shard_map/ppermute | solution.py:227
  48.9 39.4 %collective-permute-start.2 = (bf16[2,2,4,25,576]{4,2,3,1,0:T(4,128)(2,1)S(1)}, bf16[2,2,4,25,576]{4,2,3,1,0:T(4,128)(2,1)S(1)}, u32[]{:S(2)}, u32[]{:S(2)}) collective-permute-start(bf16[2,2,4,25,576]{4,2,3,1,0:T(4,128)(2,1)S(1)} %copy.120), channel_id=1, source_target_pairs={{0,4},{4,0},{8,12},{12,8},{16,20},{20,16},{24,28},{28,24},{1,5},{5... | collective-permute-start | bytes 1382408 | tf_op jit(solution)/shard_map/ppermute | solution.py:180
  81.4 41.3 %collective-permute-start.5 = (bf16[1,512,768]{2,1,0:T(8,128)(2,1)}, bf16[1,512,768]{2,1,0:T(8,128)(2,1)}, u32[]{:S(2)}, u32[]{:S(2)}) collective-permute-start(bf16[1,512,768]{2,1,0:T(8,128)(2,1)} %collective-permute-done.4), channel_id=1, source_target_pairs={{1,0},{2,1},{3,2},{5,4},{6,5},{7,6},{9,8},{10,9},{11,10},{13,12},{... | collective-permute-start | bytes 2359304 | tf_op jit(solution)/shard_map/ppermute | solution.py:228
  82.7 41.3 %collective-permute-start.7 = (bf16[1,512,768]{2,1,0:T(8,128)(2,1)}, bf16[1,512,768]{2,1,0:T(8,128)(2,1)}, u32[]{:S(2)}, u32[]{:S(2)}) collective-permute-start(bf16[1,512,768]{2,1,0:T(8,128)(2,1)} %collective-permute-done.3), channel_id=1, source_target_pairs={{0,1},{1,2},{2,3},{4,5},{5,6},{6,7},{8,9},{9,10},{10,11},{12,13},{... | collective-permute-start | bytes 2359304 | tf_op jit(solution)/shard_map/ppermute | solution.py:227
  122.8 27.5 %collective-permute-start.6 = (bf16[1,512,768]{2,1,0:T(8,128)(2,1)}, bf16[1,512,768]{2,1,0:T(8,128)(2,1)S(1)}, u32[]{:S(2)}, u32[]{:S(2)}) collective-permute-start(bf16[1,512,768]{2,1,0:T(8,128)(2,1)} %collective-permute-done.5), channel_id=1, source_target_pairs={{1,0},{2,1},{3,2},{5,4},{6,5},{7,6},{9,8},{10,9},{11,10},{13,12},{... | collective-permute-start | bytes 2359304 | tf_op jit(solution)/shard_map/ppermute | solution.py:228
  124.1 27.7 %collective-permute-start.8 = (bf16[1,512,768]{2,1,0:T(8,128)(2,1)}, bf16[1,512,768]{2,1,0:T(8,128)(2,1)S(1)}, u32[]{:S(2)}, u32[]{:S(2)}) collective-permute-start(bf16[1,512,768]{2,1,0:T(8,128)(2,1)} %collective-permute-done.7), channel_id=1, source_target_pairs={{0,1},{1,2},{2,3},{4,5},{5,6},{6,7},{8,9},{9,10},{10,11},{12,13},{... | collective-permute-start | bytes 2359304 | tf_op jit(solution)/shard_map/ppermute | solution.py:227
  154.0 2.4 copy-start.42
  154.7 1.6 copy-start.12
  201.4 6.0 %copy-start.3 = (bf16[1,512,768]{2,1,0:T(8,128)(2,1)S(1)}, bf16[1,512,768]{2,1,0:T(8,128)(2,1)}, u32[]{:S(2)}) copy-start(bf16[1,512,768]{2,1,0:T(8,128)(2,1)} %param.22) | copy-start | bytes 2359300
  203.7 16.9 %all-to-all-start.1 = ((bf16[4,512,192]{1,2,0:T(8,128)(2,1)}), bf16[4,512,192]{1,2,0:T(8,128)(2,1)S(1)}, u32[]{:S(2)}, u32[]{:S(2)}) async-start(bf16[4,512,192]{1,2,0:T(8,128)(2,1)} %copy.126), calls=%async_computation.1 | async-start | bytes 1572864 | tf_op jit(solution)/shard_map/all_to_all | solution.py:236
  207.4 311.5 %reduce-scatter.2.cloned.1.call-start = ((), (), s32[]{:S(2)}) async-start(), calls=%async_computation.6 | async-start | bytes 11354112 | tf_op jit(solution)/shard_map/reduce_scatter | solution.py:392
  228.4 30.6 %copy-start.11 = (bf16[32,96,768]{2,1,0:T(8,128)(2,1)}, bf16[32,96,768]{2,1,0:T(8,128)(2,1)S(1)}, u32[]{:S(2)}) copy-start(bf16[32,96,768]{2,1,0:T(8,128)(2,1)S(1)} %slice.306) | copy-start | bytes 14155780
  235.7 1.4 copy-start.17
  235.7 1.8 copy-start.19
  235.7 2.1 copy-start.21
  235.7 2.5 copy-start.23
  236.7 22.3 %copy-start.6 = (f32[512,768]{1,0:T(8,128)}, f32[512,768]{1,0:T(8,128)S(1)}, u32[]{:S(2)}) copy-start(f32[512,768]{1,0:T(8,128)S(1)} %get-tuple-element.111) | copy-start | bytes 4718596
  259.0 5.1 copy-start.1
  264.0 10.8 %slice-start.2 = ((s8[6291456]{0:T(1024)(128)(4,1)}), s8[2097152]{0:T(1024)(128)(4,1)S(1)}, s32[]{:S(2)}) async-start(s8[6291456]{0:T(1024)(128)(4,1)} %bitcast.223), calls=%async_computation.10 | async-start | bytes 4194304
  267.3 7.5 %slice-start = ((s8[6291456]{0:T(1024)(128)(4,1)}), s8[4194304]{0:T(1024)(128)(4,1)S(1)}, s32[]{:S(2)}) async-start(s8[6291456]{0:T(1024)(128)(4,1)} %bitcast.221), calls=%async_computation.8 | async-start | bytes 8388608
  267.3 7.5 %slice-start.1 = ((s8[6291456]{0:T(1024)(128)(4,1)}), s8[2097152]{0:T(1024)(128)(4,1)S(1)}, s32[]{:S(2)}) async-start(s8[6291456]{0:T(1024)(128)(4,1)} %bitcast.221), calls=%async_computation.9 | async-start | bytes 4194304
  267.3 8.8 %slice-start.3 = ((s8[6291456]{0:T(1024)(128)(4,1)}), s8[4194304]{0:T(1024)(128)(4,1)S(1)}, s32[]{:S(2)}) async-start(s8[6291456]{0:T(1024)(128)(4,1)} %bitcast.223), calls=%async_computation.11 | async-start | bytes 8388608
  276.1 8.6 %copy-start.7 = (f32[512,768]{1,0:T(8,128)S(1)}, f32[512,768]{1,0:T(8,128)}, u32[]{:S(2)}) copy-start(f32[512,768]{1,0:T(8,128)} %copy-done.6) | copy-start | bytes 4718596
  276.1 8.6 %copy-start.18 = (bf16[32,24,768]{2,1,0:T(8,128)(2,1)S(1)}, bf16[32,24,768]{2,1,0:T(8,128)(2,1)}, u32[]{:S(2)}) copy-start(bf16[32,24,768]{2,1,0:T(8,128)(2,1)} %copy-done.17) | copy-start | bytes 3538948
  276.1 8.6 %copy-start.20 = (bf16[32,24,768]{2,1,0:T(8,128)(2,1)S(1)}, bf16[32,24,768]{2,1,0:T(8,128)(2,1)}, u32[]{:S(2)}) copy-start(bf16[32,24,768]{2,1,0:T(8,128)(2,1)} %copy-done.19) | copy-start | bytes 3538948
  276.1 8.6 %copy-start.22 = (bf16[32,24,768]{2,1,0:T(8,128)(2,1)S(1)}, bf16[32,24,768]{2,1,0:T(8,128)(2,1)}, u32[]{:S(2)}) copy-start(bf16[32,24,768]{2,1,0:T(8,128)(2,1)} %copy-done.21) | copy-start | bytes 3538948
  276.1 8.6 %copy-start.24 = (bf16[32,24,768]{2,1,0:T(8,128)(2,1)S(1)}, bf16[32,24,768]{2,1,0:T(8,128)(2,1)}, u32[]{:S(2)}) copy-start(bf16[32,24,768]{2,1,0:T(8,128)(2,1)} %copy-done.23) | copy-start | bytes 3538948
  296.3 9.0 %copy-start.4 = (bf16[1,512,768]{2,1,0:T(8,128)(2,1)S(1)}, bf16[1,512,768]{2,1,0:T(8,128)(2,1)}, u32[]{:S(2)}) copy-start(bf16[1,512,768]{2,1,0:T(8,128)(2,1)} %param.22) | copy-start | bytes 2359300
  306.6 4.3 copy-start.9
  306.6 4.3 copy-start.26
  313.4 4.7 slice-start.4
  313.4 4.7 slice-start.5
  313.5 4.7 copy-start.25
  391.1 83.6 %all-to-all-start.3 = ((bf16[4,512,576]{1,2,0:T(8,128)(2,1)}), bf16[4,512,576]{1,2,0:T(8,128)(2,1)}, u32[]{:S(2)}, u32[]{:S(2)}) async-start(bf16[4,512,576]{1,2,0:T(8,128)(2,1)} %copy.130), calls=%async_computation.3 | async-start | bytes 4718592 | tf_op jit(solution)/shard_map/all_to_all | solution.py:236
  477.9 2.5 copy-start.15
  477.9 2.5 copy-start.27
  480.4 1.3 copy-start.10
  480.5 1.5 copy-start.13
  483.1 1.1 copy-start.2
  486.6 2.2 collective-permute-start.9
  486.7 4.9 copy-start.8
  490.1 9.8 %collective-permute-start.10 = (bf16[2,4,25,576]{3,2,1,0:T(8,128)(2,1)S(1)}, bf16[2,4,25,576]{3,2,1,0:T(8,128)(2,1)S(1)}, u32[]{:S(2)}, u32[]{:S(2)}) collective-permute-start(bf16[2,4,25,576]{3,2,1,0:T(8,128)(2,1)S(1)} %fusion.63), channel_id=1, source_target_pairs={{0,16},{4,20},{8,24},{12,28},{16,0},{20,4},{24,8},{28,12},{1,17},{... | collective-permute-start | bytes 691208 | tf_op jit(solution)/shard_map/ppermute | solution.py:180
  498.4 11.1 %copy-start.5 = (bf16[1,512,768]{2,1,0:T(8,128)(2,1)S(1)}, bf16[1,512,768]{2,1,0:T(8,128)(2,1)}, u32[]{:S(2)}) copy-start(bf16[1,512,768]{2,1,0:T(8,128)(2,1)} %param.22) | copy-start | bytes 2359300
  500.0 5.5 %collective-permute-start.11 = (bf16[4,25,576]{2,1,0:T(8,128)(2,1)S(1)}, bf16[4,25,576]{2,1,0:T(8,128)(2,1)S(1)}, u32[]{:S(2)}, u32[]{:S(2)}) collective-permute-start(bf16[4,25,576]{2,1,0:T(8,128)(2,1)S(1)} %fusion.65), channel_id=1, source_target_pairs={{0,8},{4,12},{8,0},{12,4},{16,24},{20,28},{24,16},{28,20},{1,9},{5... | collective-permute-start | bytes 345608 | tf_op jit(solution)/shard_map/ppermute | solution.py:180
  506.2 9.3 %all-to-all-start.4 = ((bf16[4,25,576]{2,1,0:T(8,128)(2,1)}), bf16[4,25,576]{2,1,0:T(8,128)(2,1)S(1)}, u32[]{:S(2)}, u32[]{:S(2)}) async-start(bf16[4,25,576]{2,1,0:T(8,128)(2,1)} %fusion.64), calls=%async_computation.4 | async-start | bytes 327680 | tf_op jit(solution)/shard_map/all_to_all | solution.py:236
  519.0 3.7 copy-start.14
  (2 other events, 1.8 us)
Sparse Core Ops, SparseCore 0:
  15.4 134.6 all-gather.2
  323.6 167.5 reduce-scatter.1
